TPU v7x, 32 devices: a whole 2x2x4 slice. The times are simulated.
32 devices in a mesh: days: 2 (over x), blk: 16 (over z, y, core).
Axes of the slice: x: 2, y: 2, z: 4, core: 2. Of those that a mesh axis runs over, the one named last changes fastest.
Arguments:
- traces: bfloat16 [2048, 8, 1024], P(('days', 'blk')), parts along dimension 0, may hold values from -6 to 6
- valid: int32 [32, 8], P(('days', 'blk')), parts along dimension 0, may hold values from 0 to 1, as said below
Outputs:
- correlations: bfloat16 [2, 32, 64, 64, 512], P(None, ('days', 'blk')), parts along dimension 1
There are 2 independent parts, one for each index of `days`. A program takes and returns all parts, laid end to end along the dimension named above; each array names one. Nothing has to cross between parts.
Inputs may be any that keep to these rules, and one draw needn't show every extreme that they name: `valid`: in every draw one block, which one is drawn from the seed, has no usable window at all.
All inputs are finite; a program needn't handle non-finite values.
Results may differ from a plain program's by a relative error of at most 0.0089.
Values may be sent and summed in bfloat16 or wider, within the bound.
A program may use at most 128 MiB of HBM per device.

v0:
```python
import math

import jax
import jax.numpy as jnp
from jax import lax
from jax.sharding import PartitionSpec as P

CH = 64
WINDOW_SAMPLES = 1024
LAGS = 512
BAND = 64
ROUNDS = 2
TIME_WINDOWS = 8
FREQS = 512


epsilon = 1e-05


def passed_along(block, axis, distance):
    devices = range(lax.axis_size(axis))
    route = [(i - distance, i) for i in devices if i - distance in devices]
    return lax.ppermute(block, axis, route)


def from_behind(block, axis, distance):
    devices = range(lax.axis_size(axis))
    route = [((i - distance) % len(devices), i) for i in devices]
    return lax.ppermute(block, axis, route)


def forward_twiddles():
    samples = jnp.arange(WINDOW_SAMPLES, dtype=jnp.int32)
    bins = jnp.arange(FREQS, dtype=jnp.int32)
    phase = (samples[:, None] * bins[None, :] % WINDOW_SAMPLES).astype(jnp.float32) * (
        2.0 * math.pi / WINDOW_SAMPLES
    )
    table = jnp.concatenate([jnp.cos(phase), -jnp.sin(phase)], axis=1) / math.sqrt(WINDOW_SAMPLES)
    return table.astype(jnp.bfloat16)


def inverse_table():
    bins = jnp.arange(FREQS, dtype=jnp.int32)
    shifts = jnp.arange(LAGS, dtype=jnp.int32) - LAGS // 2
    phase = (bins[:, None] * shifts[None, :] % WINDOW_SAMPLES).astype(jnp.float32) * (
        2.0 * math.pi / WINDOW_SAMPLES
    )
    weight = jnp.where(bins == 0, 1.0, 2.0).astype(jnp.float32)[:, None] / math.sqrt(FREQS)
    table = jnp.concatenate([weight * jnp.cos(phase), -weight * jnp.sin(phase)], axis=0)
    return table.astype(jnp.bfloat16)


def whiten(traces, prior_sample, flags):
    pair_count = traces.shape[0]
    differenced_traces = (traces.astype(jnp.float32) - prior_sample.astype(jnp.float32)).astype(
        jnp.bfloat16
    )
    window_spectra = jnp.dot(
        differenced_traces.reshape(pair_count * TIME_WINDOWS, WINDOW_SAMPLES),
        forward_twiddles(),
        preferred_element_type=jnp.float32,
    )
    window_spectra = window_spectra.reshape(pair_count, TIME_WINDOWS, 2 * FREQS)
    power = window_spectra[:, :, :FREQS] ** 2 + window_spectra[:, :, FREQS:] ** 2
    banded = jnp.mean(power.reshape(pair_count, TIME_WINDOWS, FREQS // BAND, BAND), axis=-1)
    factor = jnp.repeat(lax.rsqrt(banded + epsilon), BAND, axis=-1) * flags[:, :, None]
    return (window_spectra * jnp.concatenate([factor, factor], axis=-1)).astype(jnp.bfloat16)


def correlate(own, partner, own_flags, partner_flags, inverse_parts):
    own_real = own[:, :, :FREQS]
    own_imag = own[:, :, FREQS:]
    far_real = partner[:, :, :FREQS]
    far_imag = partner[:, :, FREQS:]
    left_side = jnp.concatenate([own_real, own_imag], axis=1)
    real_rows = jnp.concatenate([far_real, far_imag], axis=1)
    imag_rows = jnp.concatenate([far_imag, -far_real], axis=1)
    right_side = jnp.concatenate([real_rows, imag_rows], axis=0)
    cross = jnp.einsum("iuf,kuf->fik", left_side, right_side, preferred_element_type=jnp.float32)
    total = jnp.maximum(jnp.sum(own_flags * partner_flags), 1.0)
    stacked = (cross / total).astype(jnp.bfloat16).reshape(FREQS, CH, 2, CH)
    result = lax.dot_general(
        stacked, inverse_parts, (((0, 2), (1, 0)), ((), ())), preferred_element_type=jnp.float32
    )
    return result.astype(jnp.bfloat16)


def shards(traces, valid):
    last_row = traces[CH - 1 :]
    before = passed_along(last_row, "blk", 1)
    prior_sample = jnp.concatenate([before, traces[:-1]], axis=0)
    own_flags = valid.astype(jnp.float32)
    whitened = whiten(traces, prior_sample, jnp.broadcast_to(own_flags, (CH, TIME_WINDOWS)))
    flag_wire = valid.astype(jnp.bfloat16)
    inverse_parts = inverse_table().reshape(2, FREQS, LAGS)
    held = (whitened, flag_wire)
    results = []
    for round_index in range(1, ROUNDS + 1):
        held = from_behind((whitened, flag_wire), "blk", -round_index)
        results.append(
            correlate(
                whitened, held[0], own_flags[0], held[1][0].astype(jnp.float32), inverse_parts
            )
        )
    return jnp.stack(results, axis=0)[:, None]


def solution(mesh):
    return jax.shard_map(
        shards,
        mesh=mesh,
        in_specs=(P(("days", "blk"), None, None), P(("days", "blk"), None)),
        out_specs=P(None, ("days", "blk"), None, None, None),
        check_vma=False,
    )
```

profile of v0, /device:TPU:1, one launch (start us, length us, event | category | flops | bytes accessed | tf_op | source)
XLA Modules:
  0.0 117.8 jit_solution(2148790233332401265)
XLA Ops:
  0.0 0.7 convert_bitcast_fusion
  0.7 0.0 collective-permute-start.2
  0.8 5.8 %collective-permute-start.4 = (bf16[1,8]{1,0:T(2,128)(2,1)S(1)}, bf16[1,8]{1,0:T(2,128)(2,1)S(1)}, u32[]{:S(2)}, u32[]{:S(2)}) collective-permute-start(bf16[1,8]{1,0:T(2,128)(2,1)S(1)} %get-tuple-element.18), channel_id=1, source_target_pairs={{2,0},{3,1},{4,2},{5,3},{6,4},{7,5},{8,6},{9,7},{10,8},{11,9},{12,... | collective-permute-start | bytes 56 | tf_op jit(solution)/shard_map/ppermute | solution.py:29
  6.5 0.7 slice.32
  7.2 0.0 copy-start.4
  7.2 0.0 slice-start
  7.2 3.4 %collective-permute-start = (bf16[1,8,1024]{2,1,0:T(8,128)(2,1)S(1)}, bf16[1,8,1024]{2,1,0:T(8,128)(2,1)S(1)}, u32[]{:S(2)}, u32[]{:S(2)}) collective-permute-start(bf16[1,8,1024]{2,1,0:T(8,128)(2,1)S(1)} %slice.32), channel_id=1, source_target_pairs={{0,1},{1,2},{2,3},{3,4},{4,5},{5,6},{6,7},{7,8},{8,9},{9,10},{10,1... | collective-permute-start | bytes 49160 | tf_op jit(solution)/shard_map/ppermute | solution.py:23
  10.6 8.2 %sine_negate_fusion = (f32[1024,512]{1,0:T(8,128)S(1)}, f32[1024,512]{1,0:T(8,128)S(1)}) fusion(), kind=kLoop, calls=%fused_computation.22 | loop fusion | flops 7864320 | bytes 4194304 | tf_op jit(solution)/shard_map/neg | solution.py:38
  18.9 0.0 collective-permute-done
  18.9 0.0 copy-done.4
  18.9 0.0 slice-done
  18.9 1.3 %fusion.7 = f32[64,8,1024]{2,1,0:T(8,128)S(1)} fusion(f32[1024,512]{1,0:T(8,128)S(1)} %get-tuple-element.19, f32[1024,512]{1,0:T(8,128)S(1)} %get-tuple-element.20, bf16[64,8,1024]{2,1,0:T(8,128)(2,1)S(1)} %copy-done.4, bf16[63,8,1024]{2,1,0:T(8,128)(2,1)S(1)} %slice-done, bf16[1,8,1024]{2,1,0:T(8,128)(2,1)S(1)} %collective-permute-done), kind=kOutput, calls=%fused_computation.16 | convolution fusion | flops 1079508992 | bytes 8388608 | tf_op jit(solution)/shard_map/dot_general | solution.py:58
  20.2 0.0 copy-start.1
  20.2 1.3 %copy-done.1 = f32[64,8,1024]{2,1,0:T(8,128)} copy-done((f32[64,8,1024]{2,1,0:T(8,128)}, f32[64,8,1024]{2,1,0:T(8,128)S(1)}, u32[]{:S(2)}) %copy-start.1) | copy-done | bytes 2097176
  21.5 0.2 fusion.17
  21.7 0.4 reshape.39
  22.1 0.6 reduce_sum.27
  22.8 0.1 copy.25
  22.9 0.1 copy.26
  23.1 0.6 broadcast_in_dim.19
  23.7 0.7 reshape.40
  24.4 0.0 copy-start.2
  24.4 0.2 broadcast_multiply_fusion
  24.6 1.4 %copy-done.2 = f32[64,8,1024]{2,1,0:T(8,128)S(1)} copy-done((f32[64,8,1024]{2,1,0:T(8,128)S(1)}, f32[64,8,1024]{2,1,0:T(8,128)}, u32[]{:S(2)}) %copy-start.2) | copy-done | bytes 2097176
  25.9 0.5 fusion.9
  26.4 0.0 copy-start.5
  26.5 0.1 collective-permute-start.1
  26.5 4.4 %multiply_convert_fusion.1 = (bf16[512,512]{1,0:T(8,128)(2,1)S(1)}, bf16[512,512]{1,0:T(8,128)(2,1)S(1)}) fusion(s32[512]{0:T(512)S(1)} %iota_add_fusion, f32[512]{0:T(512)S(1)} %get-tuple-element.21, f32[512]{0:T(512)S(1)} %get-tuple-element.22), kind=kLoop, calls=%fused_computation.42 | loop fusion | flops 4718592 | bytes 1054720 | tf_op jit(solution)/shard_map/convert.2
  31.0 1.0 pad_maximum_fusion.1
  32.0 0.0 collective-permute-done.2
  32.0 0.0 collective-permute-done.4
  32.0 0.0 copy-done.5
  32.0 0.6 fusion.27
  34.0 0.1 collective-permute-start.3
  34.0 0.1 fusion.33
  34.1 0.1 pad_maximum_fusion
  34.2 3.5 %copy.27 = bf16[64,16,512]{0,1,2:T(8,128)(2,1)} copy(bf16[64,16,512]{2,1,0:T(8,128)(2,1)S(1)} %pad_maximum_fusion) | data formatting | bytes 2097152 | tf_op jit(solution)/shard_map/concatenate | solution.py:75
  37.7 7.3 %collective-permute-done.1 = bf16[64,8,1024]{2,1,0:T(8,128)(2,1)S(1)} collective-permute-done((bf16[64,8,1024]{2,1,0:T(8,128)(2,1)S(1)}, bf16[64,8,1024]{2,1,0:T(8,128)(2,1)S(1)}, u32[]{:S(2)}, u32[]{:S(2)}) %collective-permute-start.1) | collective-permute-done | bytes 1048608 | tf_op jit(solution)/shard_map/ppermute | solution.py:29
  45.0 0.1 fusion.31
  45.1 0.2 maximum_maximum_fusion
  45.4 3.9 %copy.28 = bf16[128,16,512]{0,1,2:T(8,128)(2,1)} copy(bf16[128,16,512]{2,1,0:T(8,128)(2,1)S(1)} %maximum_maximum_fusion) | data formatting | bytes 4194304 | tf_op jit(solution)/shard_map/concatenate | solution.py:78
  49.3 8.2 %divide_convert_fusion.1 = bf16[512,64,128]{2,1,0:T(8,128)(2,1)} fusion(f32[]{:T(128)S(6)} %max.6, bf16[64,16,512]{0,1,2:T(8,128)(2,1)} %copy.27, bf16[128,16,512]{0,1,2:T(8,128)(2,1)} %copy.28), kind=kOutput, calls=%fused_computation.1 | convolution fusion | flops 142606336 | bytes 11534340 | tf_op jit(solution)/shard_map/iuf,kuf->fik/dot_general | solution.py:79
  57.5 12.9 %copy.29 = bf16[512,64,128]{0,2,1:T(8,128)(2,1)} copy(bf16[512,64,128]{2,1,0:T(8,128)(2,1)} %divide_convert_fusion.1) | data formatting | bytes 16777216 | tf_op jit(solution)/shard_map/convert_element_type | solution.py:81
  70.4 0.0 collective-permute-done.3
  70.4 1.3 %fusion.32 = (bf16[64,8,512]{2,1,0:T(8,128)(2,1)S(1)}, bf16[64,8,512]{2,1,0:T(8,128)(2,1)S(1)}, bf16[64,8,512]{2,1,0:T(8,128)(2,1)S(1)}) fusion(bf16[64,8,1024]{2,1,0:T(8,128)(2,1)} %collective-permute-done.3), kind=kLoop, calls=%fused_computation.64 | loop fusion | flops 262144 | bytes 2621440 | tf_op jit(solution)/shard_map/slice | solution.py:73
  71.7 0.2 maximum_maximum_fusion.1
  71.9 3.9 %copy.31 = bf16[128,16,512]{0,1,2:T(8,128)(2,1)} copy(bf16[128,16,512]{2,1,0:T(8,128)(2,1)S(1)} %maximum_maximum_fusion.1) | data formatting | bytes 4194304 | tf_op jit(solution)/shard_map/concatenate | solution.py:78
  75.8 8.2 %divide_convert_fusion = bf16[512,64,128]{2,1,0:T(8,128)(2,1)} fusion(f32[]{:T(128)S(6)} %max.7, bf16[64,16,512]{0,1,2:T(8,128)(2,1)} %copy.27, bf16[128,16,512]{0,1,2:T(8,128)(2,1)} %copy.31), kind=kOutput, calls=%fused_computation | convolution fusion | flops 142606336 | bytes 11534340 | tf_op jit(solution)/shard_map/iuf,kuf->fik/dot_general | solution.py:79
  84.0 0.0 copy-start.3
  84.0 12.8 %copy.32 = bf16[512,64,128]{0,2,1:T(8,128)(2,1)} copy(bf16[512,64,128]{2,1,0:T(8,128)(2,1)} %divide_convert_fusion) | data formatting | bytes 16777216 | tf_op jit(solution)/shard_map/convert_element_type | solution.py:81
  96.9 0.0 copy-done.3
  96.9 0.0 copy-start
  96.9 8.3 %fusion = bf16[1,64,64,512]{3,2,1,0:T(8,128)(2,1)S(1)} fusion(bf16[512,64,2,64]{0,3,2,1:T(8,128)(2,1)} %bitcast.48, bf16[2,512,512,1]{2,1,0,3:T(8,128)(2,1)S(1)} %bitcast.50), kind=kOutput, calls=%fused_computation.5 | convolution fusion | flops 4297064448 | bytes 13631488 | tf_op jit(solution)/shard_map/dot_general | solution.py:82
  105.1 0.0 copy-done
  105.1 6.4 %fusion.1 = bf16[1,64,64,512]{3,2,1,0:T(8,128)(2,1)} fusion(bf16[512,64,2,64]{0,3,2,1:T(8,128)(2,1)S(1)} %bitcast.49, bf16[2,512,512,1]{2,1,0,3:T(8,128)(2,1)S(1)} %bitcast.51), kind=kOutput, calls=%fused_computation.6 | convolution fusion | flops 4297064448 | bytes 13631488 | tf_op jit(solution)/shard_map/dot_general | solution.py:82
  111.5 6.3 %maximum_bitcast_fusion = bf16[2,1,64,64,512]{4,3,2,1,0:T(8,128)(2,1)} fusion(bf16[1,64,64,512]{3,2,1,0:T(8,128)(2,1)} %fusion.1, bf16[1,64,64,512]{3,2,1,0:T(8,128)(2,1)S(1)} %fusion), kind=kLoop, calls=%fused_computation.2 | loop fusion | flops 4194304 | bytes 16777216 | tf_op jit(solution)/shard_map/broadcast_in_dim | solution.py:105
  (3 shorter events, 0.0 us)
Async XLA Ops:
  0.7 31.3 %collective-permute-start.2 = (bf16[1,8]{1,0:T(2,128)(2,1)S(1)}, bf16[1,8]{1,0:T(2,128)(2,1)S(1)}, u32[]{:S(2)}, u32[]{:S(2)}) collective-permute-start(bf16[1,8]{1,0:T(2,128)(2,1)S(1)} %get-tuple-element.18), channel_id=1, source_target_pairs={{1,0},{2,1},{3,2},{4,3},{5,4},{6,5},{7,6},{8,7},{9,8},{10,9},{11,1... | collective-permute-start | bytes 56 | tf_op jit(solution)/shard_map/ppermute | solution.py:29
  0.8 31.3 %collective-permute-start.4 = (bf16[1,8]{1,0:T(2,128)(2,1)S(1)}, bf16[1,8]{1,0:T(2,128)(2,1)S(1)}, u32[]{:S(2)}, u32[]{:S(2)}) collective-permute-start(bf16[1,8]{1,0:T(2,128)(2,1)S(1)} %get-tuple-element.18), channel_id=1, source_target_pairs={{2,0},{3,1},{4,2},{5,3},{6,4},{7,5},{8,6},{9,7},{10,8},{11,9},{12,... | collective-permute-start | bytes 56 | tf_op jit(solution)/shard_map/ppermute | solution.py:29
  7.2 11.6 %copy-start.4 = (bf16[64,8,1024]{2,1,0:T(8,128)(2,1)S(1)}, bf16[64,8,1024]{2,1,0:T(8,128)(2,1)}, u32[]{:S(2)}) copy-start(bf16[64,8,1024]{2,1,0:T(8,128)(2,1)} %param.2) | copy-start | bytes 3145732
  7.2 11.7 %slice-start = ((bf16[64,8,1024]{2,1,0:T(8,128)(2,1)}), bf16[63,8,1024]{2,1,0:T(8,128)(2,1)S(1)}, s32[]{:S(2)}) async-start(bf16[64,8,1024]{2,1,0:T(8,128)(2,1)} %param.2), calls=%async_computation | async-start | bytes 2064384 | tf_op jit(solution)/shard_map/slice | solution.py:91
  7.2 11.6 %collective-permute-start = (bf16[1,8,1024]{2,1,0:T(8,128)(2,1)S(1)}, bf16[1,8,1024]{2,1,0:T(8,128)(2,1)S(1)}, u32[]{:S(2)}, u32[]{:S(2)}) collective-permute-start(bf16[1,8,1024]{2,1,0:T(8,128)(2,1)S(1)} %slice.32), channel_id=1, source_target_pairs={{0,1},{1,2},{2,3},{3,4},{4,5},{5,6},{6,7},{7,8},{8,9},{9,10},{10,1... | collective-permute-start | bytes 49160 | tf_op jit(solution)/shard_map/ppermute | solution.py:23
  20.2 1.3 %copy-start.1 = (f32[64,8,1024]{2,1,0:T(8,128)}, f32[64,8,1024]{2,1,0:T(8,128)S(1)}, u32[]{:S(2)}) copy-start(f32[64,8,1024]{2,1,0:T(8,128)S(1)} %fusion.7) | copy-start | bytes 6291460
  24.4 1.6 %copy-start.2 = (f32[64,8,1024]{2,1,0:T(8,128)S(1)}, f32[64,8,1024]{2,1,0:T(8,128)}, u32[]{:S(2)}) copy-start(f32[64,8,1024]{2,1,0:T(8,128)} %copy-done.1) | copy-start | bytes 6291460
  26.4 5.6 %copy-start.5 = (s32[1,8]{1,0:T(1,128)S(1)}, s32[1,8]{1,0:T(1,128)}, u32[]{:S(2)}) copy-start(s32[1,8]{1,0:T(1,128)} %param.3) | copy-start | bytes 100
  26.5 18.6 %collective-permute-start.1 = (bf16[64,8,1024]{2,1,0:T(8,128)(2,1)S(1)}, bf16[64,8,1024]{2,1,0:T(8,128)(2,1)S(1)}, u32[]{:S(2)}, u32[]{:S(2)}) collective-permute-start(bf16[64,8,1024]{2,1,0:T(8,128)(2,1)S(1)} %fusion.9), channel_id=1, source_target_pairs={{1,0},{2,1},{3,2},{4,3},{5,4},{6,5},{7,6},{8,7},{9,8},{10,9},{11,1... | collective-permute-start | bytes 3145736 | tf_op jit(solution)/shard_map/ppermute | solution.py:29
  34.0 36.4 %collective-permute-start.3 = (bf16[64,8,1024]{2,1,0:T(8,128)(2,1)S(1)}, bf16[64,8,1024]{2,1,0:T(8,128)(2,1)}, u32[]{:S(2)}, u32[]{:S(2)}) collective-permute-start(bf16[64,8,1024]{2,1,0:T(8,128)(2,1)S(1)} %fusion.9), channel_id=1, source_target_pairs={{2,0},{3,1},{4,2},{5,3},{6,4},{7,5},{8,6},{9,7},{10,8},{11,9},{12,... | collective-permute-start | bytes 3145736 | tf_op jit(solution)/shard_map/ppermute | solution.py:29
  84.0 12.8 %copy-start.3 = (bf16[1024,512]{1,0:T(8,128)(2,1)S(1)}, bf16[1024,512]{1,0:T(8,128)(2,1)}, u32[]{:S(2)}) copy-start(bf16[1024,512]{1,0:T(8,128)(2,1)} %pad_maximum_fusion.1) | copy-start | bytes 3145732
  96.9 8.3 %copy-start = (bf16[512,64,128]{0,2,1:T(8,128)(2,1)S(1)}, bf16[512,64,128]{0,2,1:T(8,128)(2,1)}, u32[]{:S(2)}) copy-start(bf16[512,64,128]{0,2,1:T(8,128)(2,1)} %copy.32) | copy-start | bytes 25165828
where the time goes:
time: 119 us; the launch traced here: 118 us
  local copies, waits for them, and re-layouts  42.5 us (36%)
  matrix products  32.3 us (27%)
  other arithmetic  24.9 us (21%)
  starting transfers between devices  9.27 us (8%)
  waiting for transfers between devices  7.33 us (6%)
  between operations  1.52 us (1%)
    convert_element_type x2, local copies, waits for them, and re-layouts, correlate(): stacked = (cross / total).astype(jnp.bfloat16).reshape(FREQS, CH, 2, CH)  25.7 us
    dot_general x2, matrix products, correlate(): jnp.einsum('iuf,kuf->fik', left_side, right_side, preferred_element_type=...  16.4 us
    dot_general x2, matrix products, correlate(): lax.dot_general(stacked, inverse_parts, (((0, 2), (1, 0)), ((), ())), pre...  14.6 us
    neg x1, other arithmetic, forward_twiddles(): -jnp.sin(phase)  8.24 us
    concatenate x2, local copies, waits for them, and re-layouts, correlate(): right_side = jnp.concatenate([real_rows, imag_rows], axis=0)  7.82 us
    ppermute x4, waiting for transfers between devices, from_behind(): return lax.ppermute(block, axis, route)  7.32 us
    broadcast_in_dim x1, other arithmetic, shards(): return jnp.stack(results, axis=0)[:, None]  6.35 us
    ppermute x4, starting transfers between devices, from_behind(): return lax.ppermute(block, axis, route)  5.89 us
  transfers between devices with their start and end apart: 5, of which 1 were waited for; matrix products, arithmetic and copies ran while one was open for 41% of the time, Pallas kernels for 0%

commit v1 on v0

v1 whole, which is shorter than its diff:
```python
import functools
import math

import jax
import jax.numpy as jnp
import numpy as np
from jax import lax
from jax.experimental import pallas as pl
from jax.experimental.pallas import tpu as pltpu
from jax.sharding import PartitionSpec as P

LAGS = 512
BAND = 64
ROUNDS = 2
epsilon = 1e-05
GROUP = 8
ROWS = 8


def forward_table(samples):
    bins = samples // 2
    phase = (np.arange(bins)[:, None] * np.arange(samples)[None, :] % samples) * (
        2.0 * math.pi / samples
    )
    cos = (np.cos(phase) / math.sqrt(samples)).reshape(bins // BAND, 1, BAND, samples)
    sin = (-np.sin(phase) / math.sqrt(samples)).reshape(bins // BAND, 1, BAND, samples)
    table = np.concatenate([cos, sin], axis=1).reshape(2 * bins, samples)
    return jnp.asarray(table.astype(np.float32), dtype=jnp.bfloat16)


def inverse_table(samples):
    bins = samples // 2
    shifts = np.arange(LAGS) - LAGS // 2
    phase = (np.arange(bins)[:, None] * shifts[None, :] % samples) * (2.0 * math.pi / samples)
    weight = np.where(np.arange(bins) == 0, 1.0, 2.0)[:, None] / math.sqrt(bins)
    table = np.concatenate([weight * np.cos(phase), -weight * np.sin(phase)], axis=0)
    return jnp.asarray(table.astype(np.float32), dtype=jnp.bfloat16)


def whiten_block(x, prior, flags, table_ref, diff_ref, rows_ref, y_ref):
    ch, windows, samples = x.shape
    bins = samples // 2
    wide = x.astype(jnp.float32)
    before = jnp.concatenate([prior.astype(jnp.float32), wide[:-1]], axis=0)
    diff = (wide - before).reshape(ch * windows, samples)
    lanes = diff_ref.shape[2]
    for q in range(samples // lanes):
        diff_ref[q] = diff[:, q * lanes : (q + 1) * lanes]
        for w in range(windows):
            rows_ref[w * ch : (w + 1) * ch, q * lanes : (q + 1) * lanes] = diff_ref[
                q, pl.ds(w, ch, stride=windows), :
            ].astype(jnp.bfloat16)
    bands = 2
    height = bands * 2 * BAND
    depth = 2 * windows

    @pl.loop(0, 2 * bins // height)
    def _(step):
        at = pl.multiple_of(step * height, height)
        product = lax.dot_general(
            table_ref[pl.ds(at, height), :],
            rows_ref[...],
            (((1,), (1,)), ((), ())),
            preferred_element_type=jnp.float32,
        )
        for k in range(bands):
            real = product[k * 2 * BAND : k * 2 * BAND + BAND]
            imag = product[k * 2 * BAND + BAND : (k + 1) * 2 * BAND]
            level = jnp.sum(real * real + imag * imag, axis=0, keepdims=True) * (1.0 / BAND)
            factor = lax.rsqrt(level + epsilon) * flags
            real = real * factor
            imag = imag * factor
            first = pl.multiple_of((step * bands + k) * BAND * depth, BAND * depth)
            for w in range(windows):
                re = real[:, w * ch : (w + 1) * ch]
                im = imag[:, w * ch : (w + 1) * ch]
                y_ref[pl.ds(first + w, BAND, stride=depth), :] = jnp.concatenate([re, im], axis=1)
                y_ref[pl.ds(first + windows + w, BAND, stride=depth), :] = jnp.concatenate(
                    [im, -re], axis=1
                )


def gather_kernel(
    n,
    x_ref,
    flag_ref,
    table_ref,
    own_ref,
    far_ref,
    scale_ref,
    own_x,
    far_x,
    last_x,
    far_flag,
    diff_ref,
    rows_ref,
    y_ref,
    copy_sem,
    send_sem,
    recv_sem,
):
    me = lax.axis_index("blk")
    ch, windows, samples = own_x.shape
    barrier = pltpu.get_barrier_semaphore()
    for step in (1, 2):
        for peer in (lax.rem(me + step, n), lax.rem(me + n - step, n)):
            pl.semaphore_signal(
                barrier, inc=1, device_id={"blk": peer}, device_id_type=pl.DeviceIdType.MESH
            )
    local = pltpu.make_async_copy(x_ref, own_x, copy_sem)
    local.start()
    pl.semaphore_wait(barrier, 4)

    def remote(src, dst, slot, peer):
        return pltpu.make_async_remote_copy(
            src_ref=src,
            dst_ref=dst,
            send_sem=send_sem.at[slot],
            recv_sem=recv_sem.at[slot],
            device_id={"blk": peer},
            device_id_type=pl.DeviceIdType.MESH,
        )

    last = remote(x_ref.at[pl.ds(ch - 1, 1)], last_x, 0, lax.rem(me + 1, n))
    last.start()
    sends = []
    for r in (1, 2):
        peer = lax.rem(me + n - r, n)
        flag = remote(flag_ref, far_flag.at[r - 1], 2 * r, peer)
        flag.start()
        body = remote(x_ref, far_x.at[r - 1], 2 * r - 1, peer)
        body.start()
        sends.append((flag, body))

    flags = flag_ref[0:1, :]
    zero_row = jnp.zeros((1, windows, samples), jnp.float32)
    local.wait()
    last.wait()
    prior = jnp.where(me == 0, zero_row, last_x[...].astype(jnp.float32))
    whiten_block(own_x[...], prior, flags, table_ref, diff_ref, rows_ref, y_ref)

    wide = GROUP * 2 * windows

    @pl.loop(0, own_ref.shape[0])
    def _(g):
        at = pl.multiple_of(g * wide, wide)
        own_ref[g] = y_ref[pl.ds(at, wide), :].T[:ch].astype(jnp.bfloat16)

    for r in (1, 2):
        flag, body = sends[r - 1]
        flag.wait()
        body.wait()
        other = far_flag[r - 1][0:1, :]
        ref = own_x if r == 1 else far_x.at[r - 2]
        row = ref[ch - 1 : ch].astype(jnp.float32)
        prior = jnp.where(lax.rem(me + r, n) == 0, zero_row, row)
        whiten_block(far_x[r - 1], prior, other, table_ref, diff_ref, rows_ref, y_ref)
        far_ref[r - 1] = y_ref[...].astype(jnp.bfloat16)
        count = jnp.sum(flags * other, axis=1, keepdims=True) * (1.0 / ch)
        scale_ref[r - 1] = jnp.broadcast_to(1.0 / jnp.maximum(count, 1.0), scale_ref.shape[1:])


def cross_kernel(own_ref, far_ref, scale_ref, inverse_ref, out_ref, t_ref):
    groups, ch, wide = own_ref.shape
    depth = wide // GROUP
    bins = groups * GROUP
    stage = pl.program_id(1)

    @pl.when(stage == 0)
    def _():
        scale = scale_ref[0][0:1, :]
        scale2 = jnp.concatenate([scale, scale], axis=1)

        @pl.loop(0, groups)
        def _(g):
            lhs = own_ref[g]
            far = far_ref[0, pl.ds(pl.multiple_of(g * wide, wide), wide), :]
            zero = jnp.zeros((depth, 2 * ch), jnp.bfloat16)
            for q in range(GROUP // 2):
                columns = []
                for h in (2 * q, 2 * q + 1):
                    parts = [zero] * GROUP
                    parts[h] = far[h * depth : (h + 1) * depth]
                    columns.append(jnp.concatenate(parts, axis=0))
                rhs = jnp.concatenate(columns, axis=1)
                cross = jnp.dot(lhs, rhs, preferred_element_type=jnp.float32) * scale2
                for s in (0, 1):
                    at = pl.multiple_of((g * GROUP + 2 * q + s) * ch, ch)
                    t_ref[pl.ds(at, ch), :] = cross[:, s * 2 * ch : (s + 1) * 2 * ch]

    @pl.when(stage > 0)
    def _():
        rows = out_ref.shape[1]
        per = 4

        @pl.loop(0, rows // per)
        def _(p):
            stacked = []
            for k in range(per):
                i = (stage - 1) * rows + p * per + k
                block = t_ref[pl.ds(i, bins, stride=ch), :].astype(jnp.bfloat16).T
                stacked.append(jnp.concatenate([block[:ch], block[ch:]], axis=1))
            lhs = jnp.concatenate(stacked, axis=0)
            result = jnp.dot(lhs, inverse_ref[...], preferred_element_type=jnp.float32)
            result = result.astype(jnp.bfloat16).reshape(per, ch, result.shape[1])
            out_ref[0, pl.ds(p * per, per)] = result


def shards(traces, valid):
    n = lax.axis_size("blk")
    ch, windows, samples = traces.shape
    bins = samples // 2
    depth = 2 * windows
    vmem = pl.BlockSpec(memory_space=pltpu.VMEM)
    flags = jnp.broadcast_to(
        jnp.repeat(valid.astype(jnp.float32), ch, axis=1), (8, ch * windows)
    )
    own, far, scale = pl.pallas_call(
        functools.partial(gather_kernel, n),
        out_shape=(
            jax.ShapeDtypeStruct((bins // GROUP, ch, GROUP * depth), jnp.bfloat16),
            jax.ShapeDtypeStruct((ROUNDS, bins * depth, 2 * ch), jnp.bfloat16),
            jax.ShapeDtypeStruct((ROUNDS, 8, 2 * ch), jnp.float32),
        ),
        in_specs=[pl.BlockSpec(memory_space=pl.ANY), vmem, vmem],
        out_specs=(vmem, vmem, vmem),
        scratch_shapes=[
            pltpu.VMEM((ch, windows, samples), jnp.bfloat16),
            pltpu.VMEM((ROUNDS, ch, windows, samples), jnp.bfloat16),
            pltpu.VMEM((1, windows, samples), jnp.bfloat16),
            pltpu.VMEM((ROUNDS, 8, ch * windows), jnp.float32),
            pltpu.VMEM((samples // 128, ch * windows, 128), jnp.float32),
            pltpu.VMEM((ch * windows, samples), jnp.bfloat16),
            pltpu.VMEM((bins * depth, 2 * ch), jnp.float32),
            pltpu.SemaphoreType.DMA,
            pltpu.SemaphoreType.DMA((5,)),
            pltpu.SemaphoreType.DMA((5,)),
        ],
        compiler_params=pltpu.CompilerParams(
            collective_id=0, has_side_effects=True, vmem_limit_bytes=48 << 20
        ),
        name="gather_whiten",
    )(traces, flags, forward_table(samples))
    stages = 1 + ch // ROWS
    result = pl.pallas_call(
        cross_kernel,
        grid=(ROUNDS, stages),
        out_shape=jax.ShapeDtypeStruct((ROUNDS, ch, ch, LAGS), jnp.bfloat16),
        in_specs=[
            pl.BlockSpec(own.shape, lambda r, s: (0, 0, 0)),
            pl.BlockSpec((1,) + far.shape[1:], lambda r, s: (r, 0, 0)),
            pl.BlockSpec((1,) + scale.shape[1:], lambda r, s: (r, 0, 0)),
            pl.BlockSpec((2 * bins, LAGS), lambda r, s: (0, 0)),
        ],
        out_specs=pl.BlockSpec(
            (1, ROWS, ch, LAGS), lambda r, s: (r, jnp.maximum(s - 1, 0), 0, 0)
        ),
        scratch_shapes=[pltpu.VMEM((bins * ch, 2 * ch), jnp.float32)],
        compiler_params=pltpu.CompilerParams(
            dimension_semantics=("arbitrary", "arbitrary"), vmem_limit_bytes=48 << 20
        ),
        name="cross_inverse",
    )(own, far, scale, inverse_table(samples))
    return result[:, None]


def solution(mesh):
    return jax.shard_map(
        shards,
        mesh=mesh,
        in_specs=(P(("days", "blk"), None, None), P(("days", "blk"), None)),
        out_specs=P(None, ("days", "blk"), None, None, None),
        check_vma=False,
    )
```

time: 119 us -> 133 us (1.12)
  the two profiles are of different devices: /device:TPU:1 before, /device:TPU:4 now
where the time goes in v1:
time: 133 us
  Pallas kernels  128 us (96%)
  local copies, waits for them, and re-layouts  4.19 us (3%)
    pallas_call x1, Pallas kernels, shards(): pl.pallas_call(cross_kernel, grid=(ROUNDS, stages), out_shape=jax.ShapeDt...  68.5 us
    pallas_call x1, Pallas kernels, shards(): pl.pallas_call(functools.partial(gather_kernel, n), out_shape=(jax.ShapeD...  59.8 us
    unnamed x6, local copies, waits for them, and re-layouts  4.04 us

profile of v1, /device:TPU:4, one launch (start us, length us, event | category | flops | bytes accessed | tf_op | source)
XLA Modules:
  0.0 133.2 jit_solution(4837083855095907989)
XLA Ops:
  0.0 0.7 convert_bitcast_fusion
  0.7 0.1 broadcast_in_dim.13
  0.7 0.1 broadcast_in_dim.14
  0.8 0.0 copy-start
  0.8 1.6 %copy-done = bf16[1024,1024]{1,0:T(8,128)(2,1)S(1)} copy-done((bf16[1024,1024]{1,0:T(8,128)(2,1)S(1)}, bf16[1024,1024]{1,0:T(8,128)(2,1)}, u32[]{:S(2)}) %copy-start) | copy-done | bytes 2097176
  2.4 0.0 copy-start.1
  2.4 1.2 copy-done.1
  3.6 59.8 %gather_whiten.1 = (bf16[64,64,128]{2,1,0:T(8,128)(2,1)S(1)}, bf16[2,8192,128]{2,1,0:T(8,128)(2,1)}, f32[2,8,128]{2,1,0:T(8,128)S(1)}) custom-call(bf16[64,8,1024]{2,1,0:T(8,128)(2,1)S(1)} %copy-done.1, f32[8,512]{1,0:T(8,128)S(1)} %broadcast_in_dim.15.flag_ref, bf16[1024,1024]{1,0:T(8,128)(2,1)S(1)} %copy-done), custom_call_target="tpu_custom_call" | custom-call | tf_op jit(solution)/shard_map/gather_whiten/pallas_call | solution.py:218
  63.4 0.0 copy-start.2
  63.4 1.2 copy-done.2
  64.7 68.5 %cross_inverse.1 = bf16[2,64,64,512]{3,2,1,0:T(8,128)(2,1)} custom-call(bf16[64,64,128]{2,1,0:T(8,128)(2,1)S(1)} %get-tuple-element.8.own_ref, bf16[2,8192,128]{2,1,0:T(8,128)(2,1)} %get-tuple-element.9.far_ref, f32[2,8,128]{2,1,0:T(8,128)S(1)} %get-tuple-element.10.scale_ref, bf16[1024,512]{1,0:T(8,128)(2,1)S(1)} %copy-done.2), custom_call_target="tpu_custom_call" | custom-call | tf_op jit(solution)/shard_map/cross_inverse/pallas_call | solution.py:245
  (1 shorter events, 0.0 us)
Async XLA Ops:
  0.8 1.6 %copy-start = (bf16[1024,1024]{1,0:T(8,128)(2,1)S(1)}, bf16[1024,1024]{1,0:T(8,128)(2,1)}, u32[]{:S(2)}) copy-start(bf16[1024,1024]{1,0:T(8,128)(2,1)} %constant.4.clone.table_ref) | copy-start | bytes 6291460
  2.4 1.2 copy-start.1
  63.4 1.2 copy-start.2

commit v2 on v1

--- a/solution.py
+++ b/solution.py
@@ -15,6 +15,7 @@
 epsilon = 1e-05
 GROUP = 8
 ROWS = 8
+UNROLL = 4
 
 
 def forward_table(samples):
@@ -42,17 +43,19 @@
     bins = samples // 2
     wide = x.astype(jnp.float32)
     before = jnp.concatenate([prior.astype(jnp.float32), wide[:-1]], axis=0)
-    diff = (wide - before).reshape(ch * windows, samples)
+    diff = wide - before
     lanes = diff_ref.shape[2]
+    pitch = windows + 1
     for q in range(samples // lanes):
-        diff_ref[q] = diff[:, q * lanes : (q + 1) * lanes]
+        for c in range(ch):
+            diff_ref[q, c * pitch : c * pitch + windows] = diff[c, :, q * lanes : (q + 1) * lanes]
         for w in range(windows):
             rows_ref[w * ch : (w + 1) * ch, q * lanes : (q + 1) * lanes] = diff_ref[
-                q, pl.ds(w, ch, stride=windows), :
+                q, pl.ds(w, ch, stride=pitch), :
             ].astype(jnp.bfloat16)
     bands = 2
     height = bands * 2 * BAND
-    depth = 2 * windows
+    pitch = 2 * windows + 1
 
     @pl.loop(0, 2 * bins // height)
     def _(step):
@@ -70,12 +73,12 @@
             factor = lax.rsqrt(level + epsilon) * flags
             real = real * factor
             imag = imag * factor
-            first = pl.multiple_of((step * bands + k) * BAND * depth, BAND * depth)
+            first = pl.multiple_of((step * bands + k) * BAND * pitch, BAND * pitch)
             for w in range(windows):
                 re = real[:, w * ch : (w + 1) * ch]
                 im = imag[:, w * ch : (w + 1) * ch]
-                y_ref[pl.ds(first + w, BAND, stride=depth), :] = jnp.concatenate([re, im], axis=1)
-                y_ref[pl.ds(first + windows + w, BAND, stride=depth), :] = jnp.concatenate(
+                y_ref[pl.ds(first + w, BAND, stride=pitch), :] = jnp.concatenate([re, im], axis=1)
+                y_ref[pl.ds(first + windows + w, BAND, stride=pitch), :] = jnp.concatenate(
                     [im, -re], axis=1
                 )
 
@@ -139,12 +142,20 @@
     prior = jnp.where(me == 0, zero_row, last_x[...].astype(jnp.float32))
     whiten_block(own_x[...], prior, flags, table_ref, diff_ref, rows_ref, y_ref)
 
-    wide = GROUP * 2 * windows
-
-    @pl.loop(0, own_ref.shape[0])
-    def _(g):
-        at = pl.multiple_of(g * wide, wide)
-        own_ref[g] = y_ref[pl.ds(at, wide), :].T[:ch].astype(jnp.bfloat16)
+    groups = own_ref.shape[0]
+    depth = 2 * windows
+    wide = GROUP * depth
+
+    def bins_of(g):
+        at = pl.multiple_of(g * GROUP * (depth + 1), GROUP * (depth + 1))
+        return jnp.concatenate(
+            [y_ref[pl.ds(at + h * (depth + 1), depth), :] for h in range(GROUP)], axis=0
+        )
+
+    @pl.loop(0, groups // 4)
+    def _(q):
+        for k in range(4):
+            own_ref[q * 4 + k] = bins_of(q * 4 + k).T[:ch].astype(jnp.bfloat16)
 
     for r in (1, 2):
         flag, body = sends[r - 1]
@@ -155,7 +166,14 @@
         row = ref[ch - 1 : ch].astype(jnp.float32)
         prior = jnp.where(lax.rem(me + r, n) == 0, zero_row, row)
         whiten_block(far_x[r - 1], prior, other, table_ref, diff_ref, rows_ref, y_ref)
-        far_ref[r - 1] = y_ref[...].astype(jnp.bfloat16)
+
+        @pl.loop(0, groups // 4)
+        def _(q):
+            for k in range(4):
+                g = q * 4 + k
+                at = pl.multiple_of(g * wide, wide)
+                far_ref[r - 1, pl.ds(at, wide)] = bins_of(g).astype(jnp.bfloat16)
+
         count = jnp.sum(flags * other, axis=1, keepdims=True) * (1.0 / ch)
         scale_ref[r - 1] = jnp.broadcast_to(1.0 / jnp.maximum(count, 1.0), scale_ref.shape[1:])
 
@@ -171,8 +189,7 @@
         scale = scale_ref[0][0:1, :]
         scale2 = jnp.concatenate([scale, scale], axis=1)
 
-        @pl.loop(0, groups)
-        def _(g):
+        def cross_group(g, carry):
             lhs = own_ref[g]
             far = far_ref[0, pl.ds(pl.multiple_of(g * wide, wide), wide), :]
             zero = jnp.zeros((depth, 2 * ch), jnp.bfloat16)
@@ -185,20 +202,24 @@
                 rhs = jnp.concatenate(columns, axis=1)
                 cross = jnp.dot(lhs, rhs, preferred_element_type=jnp.float32) * scale2
                 for s in (0, 1):
-                    at = pl.multiple_of((g * GROUP + 2 * q + s) * ch, ch)
+                    at = pl.multiple_of(g * GROUP * (ch + 1), GROUP * (ch + 1))
+                    at = at + (2 * q + s) * (ch + 1)
                     t_ref[pl.ds(at, ch), :] = cross[:, s * 2 * ch : (s + 1) * 2 * ch]
+            return carry
+
+        lax.fori_loop(0, groups, cross_group, 0, unroll=UNROLL)
 
     @pl.when(stage > 0)
     def _():
         rows = out_ref.shape[1]
-        per = 4
+        per = 8
 
         @pl.loop(0, rows // per)
         def _(p):
             stacked = []
             for k in range(per):
                 i = (stage - 1) * rows + p * per + k
-                block = t_ref[pl.ds(i, bins, stride=ch), :].astype(jnp.bfloat16).T
+                block = t_ref[pl.ds(i, bins, stride=ch + 1), :].astype(jnp.bfloat16).T
                 stacked.append(jnp.concatenate([block[:ch], block[ch:]], axis=1))
             lhs = jnp.concatenate(stacked, axis=0)
             result = jnp.dot(lhs, inverse_ref[...], preferred_element_type=jnp.float32)
@@ -229,9 +250,9 @@
             pltpu.VMEM((ROUNDS, ch, windows, samples), jnp.bfloat16),
             pltpu.VMEM((1, windows, samples), jnp.bfloat16),
             pltpu.VMEM((ROUNDS, 8, ch * windows), jnp.float32),
-            pltpu.VMEM((samples // 128, ch * windows, 128), jnp.float32),
+            pltpu.VMEM((samples // 128, ch * (windows + 1), 128), jnp.float32),
             pltpu.VMEM((ch * windows, samples), jnp.bfloat16),
-            pltpu.VMEM((bins * depth, 2 * ch), jnp.float32),
+            pltpu.VMEM((bins * (depth + 1), 2 * ch), jnp.float32),
             pltpu.SemaphoreType.DMA,
             pltpu.SemaphoreType.DMA((5,)),
             pltpu.SemaphoreType.DMA((5,)),
@@ -255,7 +276,7 @@
         out_specs=pl.BlockSpec(
             (1, ROWS, ch, LAGS), lambda r, s: (r, jnp.maximum(s - 1, 0), 0, 0)
         ),
-        scratch_shapes=[pltpu.VMEM((bins * ch, 2 * ch), jnp.float32)],
+        scratch_shapes=[pltpu.VMEM((bins * (ch + 1), 2 * ch), jnp.float32)],
         compiler_params=pltpu.CompilerParams(
             dimension_semantics=("arbitrary", "arbitrary"), vmem_limit_bytes=48 << 20
         ),

time: 133 us -> 83.2 us (0.63)
  the two profiles are of different devices: /device:TPU:4 before, /device:TPU:6 now
where the time goes in v2:
time: 83.2 us; the launch traced here: 82.9 us
  Pallas kernels  78 us (94%)
  local copies, waits for them, and re-layouts  4.19 us (5%)
    pallas_call x1, Pallas kernels, shards(): pl.pallas_call(functools.partial(gather_kernel, n), out_shape=(jax.ShapeD...  53 us
    pallas_call x1, Pallas kernels, shards(): pl.pallas_call(cross_kernel, grid=(ROUNDS, stages), out_shape=jax.ShapeDt...  25 us
    unnamed x6, local copies, waits for them, and re-layouts  4.04 us

profile of v2, /device:TPU:6, one launch (start us, length us, event | category | flops | bytes accessed | tf_op | source)
XLA Modules:
  0.0 82.9 jit_solution(6040915749467149158)
XLA Ops:
  0.0 0.7 convert_bitcast_fusion
  0.7 0.1 broadcast_in_dim.13
  0.7 0.1 broadcast_in_dim.14
  0.8 0.0 copy-start
  0.8 1.6 %copy-done = bf16[1024,1024]{1,0:T(8,128)(2,1)S(1)} copy-done((bf16[1024,1024]{1,0:T(8,128)(2,1)S(1)}, bf16[1024,1024]{1,0:T(8,128)(2,1)}, u32[]{:S(2)}) %copy-start) | copy-done | bytes 2097176
  2.4 0.0 copy-start.1
  2.4 1.2 %copy-done.1 = bf16[64,8,1024]{2,1,0:T(8,128)(2,1)S(1)} copy-done((bf16[64,8,1024]{2,1,0:T(8,128)(2,1)S(1)}, bf16[64,8,1024]{2,1,0:T(8,128)(2,1)}, u32[]{:S(2)}) %copy-start.1) | copy-done | bytes 1048600
  3.6 53.0 %gather_whiten.1 = (bf16[64,64,128]{2,1,0:T(8,128)(2,1)S(1)}, bf16[2,8192,128]{2,1,0:T(8,128)(2,1)}, f32[2,8,128]{2,1,0:T(8,128)S(1)}) custom-call(bf16[64,8,1024]{2,1,0:T(8,128)(2,1)S(1)} %copy-done.1, f32[8,512]{1,0:T(8,128)S(1)} %broadcast_in_dim.15.flag_ref, bf16[1024,1024]{1,0:T(8,128)(2,1)S(1)} %copy-done), custom_call_target="tpu_custom_call" | custom-call | tf_op jit(solution)/shard_map/gather_whiten/pallas_call | solution.py:239
  56.6 0.0 copy-start.2
  56.7 1.2 %copy-done.2 = bf16[1024,512]{1,0:T(8,128)(2,1)S(1)} copy-done((bf16[1024,512]{1,0:T(8,128)(2,1)S(1)}, bf16[1024,512]{1,0:T(8,128)(2,1)}, u32[]{:S(2)}) %copy-start.2) | copy-done | bytes 1048600
  57.9 25.0 %cross_inverse.1 = bf16[2,64,64,512]{3,2,1,0:T(8,128)(2,1)} custom-call(bf16[64,64,128]{2,1,0:T(8,128)(2,1)S(1)} %get-tuple-element.8.own_ref, bf16[2,8192,128]{2,1,0:T(8,128)(2,1)} %get-tuple-element.9.far_ref, f32[2,8,128]{2,1,0:T(8,128)S(1)} %get-tuple-element.10.scale_ref, bf16[1024,512]{1,0:T(8,128)(2,1)S(1)} %copy-done.2), custom_call_target="tpu_custom_call" | custom-call | tf_op jit(solution)/shard_map/cross_inverse/pallas_call | solution.py:266
  (1 shorter events, 0.0 us)
Async XLA Ops:
  0.8 1.6 %copy-start = (bf16[1024,1024]{1,0:T(8,128)(2,1)S(1)}, bf16[1024,1024]{1,0:T(8,128)(2,1)}, u32[]{:S(2)}) copy-start(bf16[1024,1024]{1,0:T(8,128)(2,1)} %constant.4.clone.table_ref) | copy-start | bytes 6291460
  2.4 1.2 %copy-start.1 = (bf16[64,8,1024]{2,1,0:T(8,128)(2,1)S(1)}, bf16[64,8,1024]{2,1,0:T(8,128)(2,1)}, u32[]{:S(2)}) copy-start(bf16[64,8,1024]{2,1,0:T(8,128)(2,1)} %x_ref.1) | copy-start | bytes 3145732
  56.6 1.2 %copy-start.2 = (bf16[1024,512]{1,0:T(8,128)(2,1)S(1)}, bf16[1024,512]{1,0:T(8,128)(2,1)}, u32[]{:S(2)}) copy-start(bf16[1024,512]{1,0:T(8,128)(2,1)} %constant.5.clone.inverse_ref) | copy-start | bytes 3145732

commit v3 on v2

v3 whole, which is shorter than its diff:
```python
import functools
import math

import jax
import jax.numpy as jnp
import numpy as np
from jax import lax
from jax.experimental import pallas as pl
from jax.experimental.pallas import tpu as pltpu
from jax.sharding import PartitionSpec as P

LAGS = 512
BAND = 64
ROUNDS = 2
epsilon = 1e-05
GROUP = 8
ROWS = 8
UNROLL = 4


def forward_table(samples):
    bins = samples // 2
    phase = (np.arange(bins)[:, None] * np.arange(samples)[None, :] % samples) * (
        2.0 * math.pi / samples
    )
    cos = (np.cos(phase) / math.sqrt(samples)).reshape(bins // BAND, 1, BAND, samples)
    sin = (-np.sin(phase) / math.sqrt(samples)).reshape(bins // BAND, 1, BAND, samples)
    table = np.concatenate([cos, sin], axis=1).reshape(2 * bins, samples)
    return jnp.asarray(table.astype(np.float32), dtype=jnp.bfloat16)


def inverse_table(samples):
    bins = samples // 2
    shifts = np.arange(LAGS) - LAGS // 2
    phase = (np.arange(bins)[:, None] * shifts[None, :] % samples) * (2.0 * math.pi / samples)
    weight = np.where(np.arange(bins) == 0, 1.0, 2.0)[:, None] / math.sqrt(bins)
    table = np.concatenate([weight * np.cos(phase), -weight * np.sin(phase)], axis=0)
    return jnp.asarray(table.astype(np.float32), dtype=jnp.bfloat16)


def whiten_block(x, prior, flags, table_ref, diff_ref, rows_ref, y_ref):
    ch, windows, samples = x.shape
    bins = samples // 2
    wide = x.astype(jnp.float32)
    before = jnp.concatenate([prior.astype(jnp.float32), wide[:-1]], axis=0)
    diff = wide - before
    lanes = diff_ref.shape[2]
    pitch = windows + 1
    for q in range(samples // lanes):
        for c in range(ch):
            diff_ref[q, c * pitch : c * pitch + windows] = diff[c, :, q * lanes : (q + 1) * lanes]
        for w in range(windows):
            rows_ref[w * ch : (w + 1) * ch, q * lanes : (q + 1) * lanes] = diff_ref[
                q, pl.ds(w, ch, stride=pitch), :
            ].astype(jnp.bfloat16)
    bands = 2
    height = bands * 2 * BAND
    pitch = 2 * windows + 1

    @pl.loop(0, 2 * bins // height)
    def _(step):
        at = pl.multiple_of(step * height, height)
        product = lax.dot_general(
            table_ref[pl.ds(at, height), :],
            rows_ref[...],
            (((1,), (1,)), ((), ())),
            preferred_element_type=jnp.float32,
        )
        for k in range(bands):
            real = product[k * 2 * BAND : k * 2 * BAND + BAND]
            imag = product[k * 2 * BAND + BAND : (k + 1) * 2 * BAND]
            level = jnp.sum(real * real + imag * imag, axis=0, keepdims=True) * (1.0 / BAND)
            factor = lax.rsqrt(level + epsilon) * flags
            real = real * factor
            imag = imag * factor
            first = pl.multiple_of((step * bands + k) * BAND * pitch, BAND * pitch)
            for w in range(windows):
                re = real[:, w * ch : (w + 1) * ch]
                im = imag[:, w * ch : (w + 1) * ch]
                y_ref[pl.ds(first + w, BAND, stride=pitch), :] = jnp.concatenate([re, im], axis=1)
                y_ref[pl.ds(first + windows + w, BAND, stride=pitch), :] = jnp.concatenate(
                    [im, -re], axis=1
                )


def flag_lanes(flag_ref, ch):
    return jnp.concatenate(
        [jnp.full((1, ch), flag_ref[0, w], jnp.float32) for w in range(flag_ref.shape[1])], axis=1
    )


def prior_row(prior_ref, first):
    row = prior_ref[...].astype(jnp.float32)
    return jnp.where(first, jnp.zeros_like(row), row)


def bins_of(y_ref, g, depth):
    at = pl.multiple_of(g * GROUP * (depth + 1), GROUP * (depth + 1))
    return jnp.concatenate(
        [y_ref[pl.ds(at + h * (depth + 1), depth), :] for h in range(GROUP)], axis=0
    )


def own_kernel(x_ref, prior_ref, flag_ref, table_ref, own_ref, diff_ref, rows_ref, y_ref):
    ch, windows, _ = x_ref.shape
    first = lax.axis_index("blk") == 0
    whiten_block(
        x_ref[...],
        prior_row(prior_ref, first),
        flag_lanes(flag_ref, ch),
        table_ref,
        diff_ref,
        rows_ref,
        y_ref,
    )

    @pl.loop(0, own_ref.shape[0] // 4)
    def _(q):
        for k in range(4):
            block = bins_of(y_ref, q * 4 + k, 2 * windows)
            own_ref[q * 4 + k] = block.T[:ch].astype(jnp.bfloat16)


def round_kernel(
    distance,
    n,
    flag_ref,
    far_flag_ref,
    x_ref,
    prior_ref,
    own_ref,
    table_ref,
    inverse_ref,
    *rest,
):
    out_ref, diff_ref, rows_ref, y_ref, t_ref = rest[-5:]
    groups, ch, wide = own_ref.shape
    windows = flag_ref.shape[1]
    depth = wide // GROUP
    bins = groups * GROUP
    stage = pl.program_id(0)

    @pl.when(stage == 0)
    def _():
        first = lax.rem(lax.axis_index("blk") + distance, n) == 0
        whiten_block(
            x_ref[...],
            prior_row(prior_ref, first),
            flag_lanes(far_flag_ref, ch),
            table_ref,
            diff_ref,
            rows_ref,
            y_ref,
        )
        count = sum(flag_ref[0, w] * far_flag_ref[0, w] for w in range(windows))
        scale = 1.0 / jnp.maximum(jnp.full((1, 4 * ch), count, jnp.float32), 1.0)

        def cross_group(g, carry):
            lhs = own_ref[g]
            far = bins_of(y_ref, g, depth).astype(jnp.bfloat16)
            zero = jnp.zeros((depth, 2 * ch), jnp.bfloat16)
            for q in range(GROUP // 2):
                columns = []
                for h in (2 * q, 2 * q + 1):
                    parts = [zero] * GROUP
                    parts[h] = far[h * depth : (h + 1) * depth]
                    columns.append(jnp.concatenate(parts, axis=0))
                rhs = jnp.concatenate(columns, axis=1)
                cross = jnp.dot(lhs, rhs, preferred_element_type=jnp.float32) * scale
                for s in (0, 1):
                    at = pl.multiple_of(g * GROUP * (ch + 1), GROUP * (ch + 1))
                    at = at + (2 * q + s) * (ch + 1)
                    t_ref[pl.ds(at, ch), :] = cross[:, s * 2 * ch : (s + 1) * 2 * ch]
            return carry

        lax.fori_loop(0, groups, cross_group, 0, unroll=UNROLL)

    @pl.when(stage > 0)
    def _():
        rows = out_ref.shape[1]
        stacked = []
        for k in range(rows):
            i = (stage - 1) * rows + k
            block = t_ref[pl.ds(i, bins, stride=ch + 1), :].astype(jnp.bfloat16).T
            stacked.append(jnp.concatenate([block[:ch], block[ch:]], axis=1))
        lhs = jnp.concatenate(stacked, axis=0)
        result = jnp.dot(lhs, inverse_ref[...], preferred_element_type=jnp.float32)
        out_ref[0] = result.astype(jnp.bfloat16).reshape(rows, ch, result.shape[1])


def shards(traces, valid):
    n = lax.axis_size("blk")
    ch, windows, samples = traces.shape
    bins = samples // 2
    depth = 2 * windows

    def behind(value, distance):
        return lax.ppermute(value, "blk", [((i + distance) % n, i) for i in range(n)])

    before = behind(traces[ch - 1 :], -1)
    blocks = [traces] + [behind(traces, r) for r in range(1, ROUNDS + 1)]
    wire = valid.astype(jnp.bfloat16)
    flags = [wire] + [behind(wire, r) for r in range(1, ROUNDS + 1)]
    flags = [f.astype(jnp.float32) for f in flags]
    table = forward_table(samples)
    inverse = inverse_table(samples)

    smem = pl.BlockSpec(memory_space=pltpu.SMEM)
    vmem = pl.BlockSpec(memory_space=pltpu.VMEM)
    scratch = [
        pltpu.VMEM((samples // 128, ch * (windows + 1), 128), jnp.float32),
        pltpu.VMEM((ch * windows, samples), jnp.bfloat16),
        pltpu.VMEM((bins * (depth + 1), 2 * ch), jnp.float32),
    ]
    dft_flops = 2 * ch * windows * samples * samples
    own = pl.pallas_call(
        own_kernel,
        out_shape=jax.ShapeDtypeStruct((bins // GROUP, ch, GROUP * depth), jnp.bfloat16),
        in_specs=[vmem, vmem, smem, vmem],
        out_specs=vmem,
        scratch_shapes=scratch,
        compiler_params=pltpu.CompilerParams(vmem_limit_bytes=48 << 20),
        cost_estimate=pl.CostEstimate(
            flops=4 * dft_flops, bytes_accessed=8 << 20, transcendentals=0
        ),
        name="whiten_own",
    )(traces, before, flags[0], table)

    stages = 1 + ch // ROWS
    once = pl.Buffered(1)
    result = None
    for r in range(1, ROUNDS + 1):
        operands = [flags[0], flags[r], blocks[r], blocks[r - 1], own, table, inverse]
        in_specs = [
            smem,
            smem,
            pl.BlockSpec((ch, windows, samples), lambda s: (0, 0, 0), pipeline_mode=once),
            pl.BlockSpec((1, windows, samples), lambda s: (ch - 1, 0, 0), pipeline_mode=once),
            pl.BlockSpec(own.shape, lambda s: (0, 0, 0), pipeline_mode=once),
            pl.BlockSpec(table.shape, lambda s: (0, 0), pipeline_mode=once),
            pl.BlockSpec(inverse.shape, lambda s: (0, 0), pipeline_mode=once),
        ]
        alias = {}
        if result is not None:
            alias = {len(operands): 0}
            operands.append(result)
            in_specs.append(pl.BlockSpec(memory_space=pl.ANY))
        result = pl.pallas_call(
            functools.partial(round_kernel, r, n),
            grid=(stages,),
            out_shape=jax.ShapeDtypeStruct((ROUNDS, ch, ch, LAGS), jnp.bfloat16),
            in_specs=in_specs,
            out_specs=pl.BlockSpec(
                (1, ROWS, ch, LAGS), lambda s, r=r: (r - 1, jnp.maximum(s - 1, 0), 0, 0)
            ),
            scratch_shapes=scratch + [pltpu.VMEM((bins * (ch + 1), 2 * ch), jnp.float32)],
            input_output_aliases=alias,
            compiler_params=pltpu.CompilerParams(vmem_limit_bytes=48 << 20),
            cost_estimate=pl.CostEstimate(
                flops=16 * dft_flops, bytes_accessed=16 << 20, transcendentals=0
            ),
            name=f"round_{r}",
        )(*operands)
    return result[:, None]


def solution(mesh):
    return jax.shard_map(
        shards,
        mesh=mesh,
        in_specs=(P(("days", "blk"), None, None), P(("days", "blk"), None)),
        out_specs=P(None, ("days", "blk"), None, None, None),
        check_vma=False,
    )
```

time: 83.2 us -> 66.3 us (0.80)
  the two profiles are of different devices: /device:TPU:6 before, /device:TPU:0 now
where the time goes in v3:
time: 66.3 us; the launch traced here: 66 us
  Pallas kernels  39.1 us (59%)
  waiting for transfers between devices  12.7 us (19%)
  starting transfers between devices  9.92 us (15%)
  local copies, waits for them, and re-layouts  3.57 us (5%)
    pallas_call x2, Pallas kernels, shards(): pl.pallas_call(functools.partial(round_kernel, r, n), grid=(stages,), out...  33.7 us
    ppermute x5, waiting for transfers between devices, behind(): lax.ppermute(value, 'blk', [((i + distance) % n, i) for i in range(n)])  12.7 us
    ppermute x5, starting transfers between devices, behind(): lax.ppermute(value, 'blk', [((i + distance) % n, i) for i in range(n)])  9.92 us
    pallas_call x1, Pallas kernels, shards(): pl.pallas_call(own_kernel, out_shape=jax.ShapeDtypeStruct((bins // GROUP,...  5.44 us
    unnamed x6, local copies, waits for them, and re-layouts  2.81 us
  transfers between devices with their start and end apart: 5, of which 1 were waited for; matrix products, arithmetic and copies ran while one was open for 2% of the time, Pallas kernels for 34%

profile of v3, /device:TPU:0, one launch (start us, length us, event | category | flops | bytes accessed | tf_op | source)
XLA Modules:
  0.0 66.0 jit_solution(11779741261958866231)
XLA Ops:
  0.0 5.5 %collective-permute-start.2 = (bf16[64,8,1024]{2,1,0:T(8,128)(2,1)}, bf16[64,8,1024]{2,1,0:T(8,128)(2,1)S(1)}, u32[]{:S(2)}, u32[]{:S(2)}) collective-permute-start(bf16[64,8,1024]{2,1,0:T(8,128)(2,1)} %prior_ref.1), channel_id=1, source_target_pairs={{1,0},{2,1},{3,2},{4,3},{5,4},{6,5},{7,6},{8,7},{9,8},{10,9},{11,1... | collective-permute-start | bytes 3145736 | tf_op jit(solution)/shard_map/ppermute | solution.py:198
  5.5 0.8 %slice.3 = bf16[1,8,1024]{2,1,0:T(8,128)(2,1)S(1)} slice(bf16[64,8,1024]{2,1,0:T(8,128)(2,1)} %prior_ref.1), slice={[63:64], [0:8], [0:1024]} | slice | bytes 32768 | tf_op jit(solution)/shard_map/slice | solution.py:200
  6.2 0.0 collective-permute-start.3
  6.2 0.7 fusion
  6.9 1.0 %collective-permute-start = (bf16[1,8]{1,0:T(2,128)(2,1)S(1)}, bf16[1,8]{1,0:T(2,128)(2,1)S(1)}, u32[]{:S(2)}, u32[]{:S(2)}) collective-permute-start(bf16[1,8]{1,0:T(2,128)(2,1)S(1)} %get-tuple-element.5), channel_id=1, source_target_pairs={{2,0},{3,1},{4,2},{5,3},{6,4},{7,5},{8,6},{9,7},{10,8},{11,9},{12,... | collective-permute-start | bytes 56 | tf_op jit(solution)/shard_map/ppermute | solution.py:198
  7.9 3.4 %collective-permute-start.4 = (bf16[1,8]{1,0:T(2,128)(2,1)S(1)}, bf16[1,8]{1,0:T(2,128)(2,1)S(1)}, u32[]{:S(2)}, u32[]{:S(2)}) collective-permute-start(bf16[1,8]{1,0:T(2,128)(2,1)S(1)} %get-tuple-element.5), channel_id=1, source_target_pairs={{1,0},{2,1},{3,2},{4,3},{5,4},{6,5},{7,6},{8,7},{9,8},{10,9},{11,1... | collective-permute-start | bytes 56 | tf_op jit(solution)/shard_map/ppermute | solution.py:198
  11.3 0.0 collective-permute-start.1
  11.3 12.7 %collective-permute-done = bf16[1,8]{1,0:T(2,128)(2,1)S(1)} collective-permute-done((bf16[1,8]{1,0:T(2,128)(2,1)S(1)}, bf16[1,8]{1,0:T(2,128)(2,1)S(1)}, u32[]{:S(2)}, u32[]{:S(2)}) %collective-permute-start) | collective-permute-done | bytes 48 | tf_op jit(solution)/shard_map/ppermute | solution.py:198
  24.0 0.0 collective-permute-done.4
  24.0 0.0 collective-permute-done.3.prior_ref
  24.0 0.0 copy-start
  24.0 1.2 %copy-done = bf16[64,8,1024]{2,1,0:T(8,128)(2,1)S(1)} copy-done((bf16[64,8,1024]{2,1,0:T(8,128)(2,1)S(1)}, bf16[64,8,1024]{2,1,0:T(8,128)(2,1)}, u32[]{:S(2)}) %copy-start) | copy-done | bytes 1048600
  25.3 0.0 copy-start.1
  25.3 1.6 %copy-done.1 = bf16[1024,1024]{1,0:T(8,128)(2,1)S(1)} copy-done((bf16[1024,1024]{1,0:T(8,128)(2,1)S(1)}, bf16[1024,1024]{1,0:T(8,128)(2,1)}, u32[]{:S(2)}) %copy-start.1) | copy-done | bytes 2097176
  26.9 0.0 copy-start.2
  26.9 5.4 %whiten_own.1.own_ref = bf16[64,64,128]{2,1,0:T(8,128)(2,1)S(1)} custom-call(bf16[64,8,1024]{2,1,0:T(8,128)(2,1)S(1)} %copy-done, bf16[1,8,1024]{2,1,0:T(8,128)(2,1)S(1)} %collective-permute-done.3.prior_ref, f32[1,8]{1,0:T(1,128)S(1)} %get-tuple-element.6.flag_ref, bf16[1024,1024]{1,0:T(8,128)(2,1)S(1)} %copy-done.1), custom_call_target="tpu_custom_call" | custom-call | flops 4294967296 | bytes 8388608 | tf_op jit(solution)/shard_map/whiten_own/pallas_call | solution.py:216
  32.3 0.0 collective-permute-done.2.x_ref.prior_ref
  32.3 0.0 copy-done.2
  32.3 16.8 %round_1.1.rest_0_ = bf16[2,64,64,512]{3,2,1,0:T(8,128)(2,1)} custom-call(f32[1,8]{1,0:T(1,128)S(1)} %get-tuple-element.6.flag_ref, f32[1,8]{1,0:T(1,128)S(1)} %convert_element_type.15.far_flag_ref, bf16[64,8,1024]{2,1,0:T(8,128)(2,1)S(1)} %collective-permute-done.2.x_ref.prior_ref, bf16[64,8,1024]{2,1,0:T(8,128)(2,1)S(1)} %copy-done, ...), custom_call_target="tpu_custom_call" | custom-call | flops 17179869184 | bytes 16777216 | tf_op jit(solution)/shard_map/round_1/pallas_call | solution.py:248
  49.2 0.0 collective-permute-done.1.x_ref
  49.2 16.8 %round_2.1 = bf16[2,64,64,512]{3,2,1,0:T(8,128)(2,1)} custom-call(f32[1,8]{1,0:T(1,128)S(1)} %get-tuple-element.6.flag_ref, f32[1,8]{1,0:T(1,128)S(1)} %convert_element_type.14.far_flag_ref, bf16[64,8,1024]{2,1,0:T(8,128)(2,1)S(1)} %collective-permute-done.1.x_ref, ...), custom_call_target="tpu_custom_call", output_to_operand_aliasing={{}: (7, {})} | custom-call | flops 17179869184 | bytes 16777216 | tf_op jit(solution)/shard_map/round_2/pallas_call | solution.py:248
  (2 shorter events, 0.0 us)
Async XLA Ops:
  0.0 32.3 %collective-permute-start.2 = (bf16[64,8,1024]{2,1,0:T(8,128)(2,1)}, bf16[64,8,1024]{2,1,0:T(8,128)(2,1)S(1)}, u32[]{:S(2)}, u32[]{:S(2)}) collective-permute-start(bf16[64,8,1024]{2,1,0:T(8,128)(2,1)} %prior_ref.1), channel_id=1, source_target_pairs={{1,0},{2,1},{3,2},{4,3},{5,4},{6,5},{7,6},{8,7},{9,8},{10,9},{11,1... | collective-permute-start | bytes 3145736 | tf_op jit(solution)/shard_map/ppermute | solution.py:198
  6.2 17.8 %collective-permute-start.3 = (bf16[1,8,1024]{2,1,0:T(8,128)(2,1)S(1)}, bf16[1,8,1024]{2,1,0:T(8,128)(2,1)S(1)}, u32[]{:S(2)}, u32[]{:S(2)}) collective-permute-start(bf16[1,8,1024]{2,1,0:T(8,128)(2,1)S(1)} %slice.3), channel_id=1, source_target_pairs={{15,0},{0,1},{1,2},{2,3},{3,4},{4,5},{5,6},{6,7},{7,8},{8,9},{9,10... | collective-permute-start | bytes 49160 | tf_op jit(solution)/shard_map/ppermute | solution.py:198
  6.9 17.1 %collective-permute-start = (bf16[1,8]{1,0:T(2,128)(2,1)S(1)}, bf16[1,8]{1,0:T(2,128)(2,1)S(1)}, u32[]{:S(2)}, u32[]{:S(2)}) collective-permute-start(bf16[1,8]{1,0:T(2,128)(2,1)S(1)} %get-tuple-element.5), channel_id=1, source_target_pairs={{2,0},{3,1},{4,2},{5,3},{6,4},{7,5},{8,6},{9,7},{10,8},{11,9},{12,... | collective-permute-start | bytes 56 | tf_op jit(solution)/shard_map/ppermute | solution.py:198
  7.9 16.1 %collective-permute-start.4 = (bf16[1,8]{1,0:T(2,128)(2,1)S(1)}, bf16[1,8]{1,0:T(2,128)(2,1)S(1)}, u32[]{:S(2)}, u32[]{:S(2)}) collective-permute-start(bf16[1,8]{1,0:T(2,128)(2,1)S(1)} %get-tuple-element.5), channel_id=1, source_target_pairs={{1,0},{2,1},{3,2},{4,3},{5,4},{6,5},{7,6},{8,7},{9,8},{10,9},{11,1... | collective-permute-start | bytes 56 | tf_op jit(solution)/shard_map/ppermute | solution.py:198
  11.3 37.8 %collective-permute-start.1 = (bf16[64,8,1024]{2,1,0:T(8,128)(2,1)}, bf16[64,8,1024]{2,1,0:T(8,128)(2,1)S(1)}, u32[]{:S(2)}, u32[]{:S(2)}) collective-permute-start(bf16[64,8,1024]{2,1,0:T(8,128)(2,1)} %prior_ref.1), channel_id=1, source_target_pairs={{2,0},{3,1},{4,2},{5,3},{6,4},{7,5},{8,6},{9,7},{10,8},{11,9},{12,... | collective-permute-start | bytes 3145736 | tf_op jit(solution)/shard_map/ppermute | solution.py:198
  24.0 1.2 %copy-start = (bf16[64,8,1024]{2,1,0:T(8,128)(2,1)S(1)}, bf16[64,8,1024]{2,1,0:T(8,128)(2,1)}, u32[]{:S(2)}) copy-start(bf16[64,8,1024]{2,1,0:T(8,128)(2,1)} %prior_ref.1) | copy-start | bytes 3145732
  25.3 1.6 %copy-start.1 = (bf16[1024,1024]{1,0:T(8,128)(2,1)S(1)}, bf16[1024,1024]{1,0:T(8,128)(2,1)}, u32[]{:S(2)}) copy-start(bf16[1024,1024]{1,0:T(8,128)(2,1)} %constant.4.clone.table_ref) | copy-start | bytes 6291460
  26.9 5.5 %copy-start.2 = (bf16[1024,512]{1,0:T(8,128)(2,1)S(1)}, bf16[1024,512]{1,0:T(8,128)(2,1)}, u32[]{:S(2)}) copy-start(bf16[1024,512]{1,0:T(8,128)(2,1)} %constant.5.clone.inverse_ref) | copy-start | bytes 3145732

commit v4 on v3

--- a/solution.py
+++ b/solution.py
@@ -15,7 +15,8 @@
 epsilon = 1e-05
 GROUP = 8
 ROWS = 8
-UNROLL = 4
+UNROLL = 16
+VMEM_BYTES = 48 << 20
 
 
 def forward_table(samples):
@@ -38,7 +39,7 @@
     return jnp.asarray(table.astype(np.float32), dtype=jnp.bfloat16)
 
 
-def whiten_block(x, prior, flags, table_ref, diff_ref, rows_ref, y_ref):
+def whiten_block(x, prior, flags, table_ref, diff_ref, rows_ref, y_ref, ready=None):
     ch, windows, samples = x.shape
     bins = samples // 2
     wide = x.astype(jnp.float32)
@@ -53,6 +54,8 @@
             rows_ref[w * ch : (w + 1) * ch, q * lanes : (q + 1) * lanes] = diff_ref[
                 q, pl.ds(w, ch, stride=pitch), :
             ].astype(jnp.bfloat16)
+    if ready is not None:
+        ready()
     bands = 2
     height = bands * 2 * BAND
     pitch = 2 * windows + 1
@@ -84,9 +87,8 @@
 
 
 def flag_lanes(flag_ref, ch):
-    return jnp.concatenate(
-        [jnp.full((1, ch), flag_ref[0, w], jnp.float32) for w in range(flag_ref.shape[1])], axis=1
-    )
+    row = flag_ref[0].astype(jnp.float32)
+    return jnp.concatenate([row[w : w + 1, :ch] for w in range(row.shape[0])], axis=1)
 
 
 def prior_row(prior_ref, first):
@@ -101,7 +103,11 @@
     )
 
 
-def own_kernel(x_ref, prior_ref, flag_ref, table_ref, own_ref, diff_ref, rows_ref, y_ref):
+def own_kernel(
+    x_ref, prior_ref, flag_ref, table_hbm, own_ref, table_ref, sem, diff_ref, rows_ref, y_ref
+):
+    fetch = pltpu.make_async_copy(table_hbm, table_ref, sem)
+    fetch.start()
     ch, windows, _ = x_ref.shape
     first = lax.axis_index("blk") == 0
     whiten_block(
@@ -112,6 +118,7 @@
         diff_ref,
         rows_ref,
         y_ref,
+        fetch.wait,
     )
 
     @pl.loop(0, own_ref.shape[0] // 4)
@@ -152,8 +159,9 @@
             rows_ref,
             y_ref,
         )
-        count = sum(flag_ref[0, w] * far_flag_ref[0, w] for w in range(windows))
-        scale = 1.0 / jnp.maximum(jnp.full((1, 4 * ch), count, jnp.float32), 1.0)
+        shared = flag_ref[0].astype(jnp.float32) * far_flag_ref[0].astype(jnp.float32)
+        count = jnp.sum(shared[:, : 4 * ch], axis=0, keepdims=True)
+        scale = 1.0 / jnp.maximum(count, 1.0)
 
         def cross_group(g, carry):
             lhs = own_ref[g]
@@ -198,15 +206,21 @@
         return lax.ppermute(value, "blk", [((i + distance) % n, i) for i in range(n)])
 
     before = behind(traces[ch - 1 :], -1)
-    blocks = [traces] + [behind(traces, r) for r in range(1, ROUNDS + 1)]
-    wire = valid.astype(jnp.bfloat16)
-    flags = [wire] + [behind(wire, r) for r in range(1, ROUNDS + 1)]
-    flags = [f.astype(jnp.float32) for f in flags]
+    row = jnp.broadcast_to(valid.astype(jnp.bfloat16)[:, :, None], (1, windows, samples))
+    tagged = jnp.concatenate([traces, row], axis=0)
+    blocks = [tagged] + [behind(tagged, r) for r in range(1, ROUNDS + 1)]
     table = forward_table(samples)
     inverse = inverse_table(samples)
 
-    smem = pl.BlockSpec(memory_space=pltpu.SMEM)
-    vmem = pl.BlockSpec(memory_space=pltpu.VMEM)
+    once = pl.Buffered(1)
+
+    def whole(shape):
+        return pl.BlockSpec(shape, lambda s: (0,) * len(shape), pipeline_mode=once)
+
+    def row_at(at):
+        return pl.BlockSpec((1, windows, samples), lambda s: (at, 0, 0), pipeline_mode=once)
+
+    block = whole((ch, windows, samples))
     scratch = [
         pltpu.VMEM((samples // 128, ch * (windows + 1), 128), jnp.float32),
         pltpu.VMEM((ch * windows, samples), jnp.bfloat16),
@@ -216,29 +230,33 @@
     own = pl.pallas_call(
         own_kernel,
         out_shape=jax.ShapeDtypeStruct((bins // GROUP, ch, GROUP * depth), jnp.bfloat16),
-        in_specs=[vmem, vmem, smem, vmem],
-        out_specs=vmem,
-        scratch_shapes=scratch,
-        compiler_params=pltpu.CompilerParams(vmem_limit_bytes=48 << 20),
+        grid=(1,),
+        in_specs=[block, row_at(0), row_at(ch), pl.BlockSpec(memory_space=pl.ANY)],
+        out_specs=whole((bins // GROUP, ch, GROUP * depth)),
+        scratch_shapes=[
+            pltpu.VMEM((2 * bins, samples), jnp.bfloat16),
+            pltpu.SemaphoreType.DMA,
+        ]
+        + scratch,
+        compiler_params=pltpu.CompilerParams(vmem_limit_bytes=VMEM_BYTES),
         cost_estimate=pl.CostEstimate(
             flops=4 * dft_flops, bytes_accessed=8 << 20, transcendentals=0
         ),
         name="whiten_own",
-    )(traces, before, flags[0], table)
+    )(traces, before, tagged, table)
 
     stages = 1 + ch // ROWS
-    once = pl.Buffered(1)
     result = None
     for r in range(1, ROUNDS + 1):
-        operands = [flags[0], flags[r], blocks[r], blocks[r - 1], own, table, inverse]
+        operands = [tagged, blocks[r], blocks[r], blocks[r - 1], own, table, inverse]
         in_specs = [
-            smem,
-            smem,
-            pl.BlockSpec((ch, windows, samples), lambda s: (0, 0, 0), pipeline_mode=once),
-            pl.BlockSpec((1, windows, samples), lambda s: (ch - 1, 0, 0), pipeline_mode=once),
-            pl.BlockSpec(own.shape, lambda s: (0, 0, 0), pipeline_mode=once),
-            pl.BlockSpec(table.shape, lambda s: (0, 0), pipeline_mode=once),
-            pl.BlockSpec(inverse.shape, lambda s: (0, 0), pipeline_mode=once),
+            row_at(ch),
+            row_at(ch),
+            block,
+            row_at(ch - 1),
+            whole(own.shape),
+            whole(table.shape),
+            whole(inverse.shape),
         ]
         alias = {}
         if result is not None:
@@ -255,7 +273,7 @@
             ),
             scratch_shapes=scratch + [pltpu.VMEM((bins * (ch + 1), 2 * ch), jnp.float32)],
             input_output_aliases=alias,
-            compiler_params=pltpu.CompilerParams(vmem_limit_bytes=48 << 20),
+            compiler_params=pltpu.CompilerParams(vmem_limit_bytes=VMEM_BYTES),
             cost_estimate=pl.CostEstimate(
                 flops=16 * dft_flops, bytes_accessed=16 << 20, transcendentals=0
             ),

time: 66.3 us -> 58.1 us (0.88)
  the two profiles are of different devices: /device:TPU:0 before, /device:TPU:1 now
where the time goes in v4:
time: 58.1 us; the launch traced here: 57 us
  Pallas kernels  34.8 us (60%)
  starting transfers between devices  9.53 us (16%)
  waiting for transfers between devices  8.85 us (15%)
  other arithmetic  2.06 us (4%)
  local copies, waits for them, and re-layouts  1.73 us (3%)
    pallas_call x2, Pallas kernels, shards(): pl.pallas_call(functools.partial(round_kernel, r, n), grid=(stages,), out...  29.7 us
    ppermute x3, starting transfers between devices, behind(): lax.ppermute(value, 'blk', [((i + distance) % n, i) for i in range(n)])  9.53 us
    ppermute x3, waiting for transfers between devices, behind(): lax.ppermute(value, 'blk', [((i + distance) % n, i) for i in range(n)])  8.85 us
    pallas_call x1, Pallas kernels, shards(): pl.pallas_call(own_kernel, out_shape=jax.ShapeDtypeStruct((bins // GROUP,...  5.07 us
    unnamed x6, local copies, waits for them, and re-layouts  1.66 us
    concatenate x1, other arithmetic, shards(): tagged = jnp.concatenate([traces, row], axis=0)  1.41 us
  transfers between devices with their start and end apart: 3, of which 1 were waited for; matrix products, arithmetic and copies ran while one was open for 0% of the time, Pallas kernels for 35%

profile of v4, /device:TPU:1, one launch (start us, length us, event | category | flops | bytes accessed | tf_op | source)
XLA Modules:
  0.0 57.0 jit_solution(17825149221158077368)
XLA Ops:
  0.0 0.7 %convert_bitcast_fusion = bf16[8]{0:T(256)(128)(2,1)S(1)} fusion(s32[1,8]{1,0:T(1,128)} %param.5), kind=kLoop, calls=%fused_computation.1 | loop fusion | flops 8 | bytes 48 | tf_op jit(solution)/shard_map/broadcast_in_dim | solution.py:209
  0.7 0.1 broadcast_in_dim.12
  0.7 0.0 copy-start
  0.7 1.4 %pad_maximum_fusion.flag_ref.prior_ref = bf16[65,8,1024]{2,1,0:T(8,128)(2,1)S(1)} fusion(bf16[1,8,1024]{2,1,0:T(8,128)(2,1)S(1)} %broadcast_in_dim.12, bf16[64,8,1024]{2,1,0:T(8,128)(2,1)} %x_ref.1), kind=kLoop, calls=%fused_computation | loop fusion | flops 532480 | bytes 2129920 | tf_op jit(solution)/shard_map/concatenate | solution.py:210
  2.1 0.1 collective-permute-start.1
  2.2 0.1 copy-done
  2.3 2.6 %collective-permute-start.2 = (bf16[1,8,1024]{2,1,0:T(8,128)(2,1)S(1)}, bf16[1,8,1024]{2,1,0:T(8,128)(2,1)S(1)}, u32[]{:S(2)}, u32[]{:S(2)}) collective-permute-start(bf16[1,8,1024]{2,1,0:T(8,128)(2,1)S(1)} %slice.3), channel_id=1, source_target_pairs={{15,0},{0,1},{1,2},{2,3},{3,4},{4,5},{5,6},{6,7},{7,8},{8,9},{9,10... | collective-permute-start | bytes 49160 | tf_op jit(solution)/shard_map/ppermute | solution.py:206
  4.9 6.8 %collective-permute-start = (bf16[65,8,1024]{2,1,0:T(8,128)(2,1)S(1)}, bf16[65,8,1024]{2,1,0:T(8,128)(2,1)S(1)}, u32[]{:S(2)}, u32[]{:S(2)}) collective-permute-start(bf16[65,8,1024]{2,1,0:T(8,128)(2,1)S(1)} %pad_maximum_fusion.flag_ref.prior_ref), channel_id=1, source_target_pairs={{2,0},{3,1},{4,2},{5,3},{6,4},{7,5},{8,6},{9,7},{10,8},{11,9},{12,... | collective-permute-start | bytes 3194888 | tf_op jit(solution)/shard_map/ppermute | solution.py:206
  11.7 0.0 collective-permute-done.2.prior_ref
  11.7 0.0 copy-start.1
  11.7 1.6 %copy-done.1 = bf16[1024,1024]{1,0:T(8,128)(2,1)S(1)} copy-done((bf16[1024,1024]{1,0:T(8,128)(2,1)S(1)}, bf16[1024,1024]{1,0:T(8,128)(2,1)}, u32[]{:S(2)}) %copy-start.1) | copy-done | bytes 2097176
  13.3 0.0 copy-start.2
  13.3 5.1 %whiten_own.1.own_ref = bf16[64,64,128]{2,1,0:T(8,128)(2,1)S(1)} custom-call(bf16[64,8,1024]{2,1,0:T(8,128)(2,1)S(1)} %copy-done, bf16[1,8,1024]{2,1,0:T(8,128)(2,1)S(1)} %collective-permute-done.2.prior_ref, bf16[65,8,1024]{2,1,0:T(8,128)(2,1)S(1)} %pad_maximum_fusion.flag_ref.prior_ref, bf16[1024,1024]{1,0:T(8,128)(2,1)S(1)} %copy-done.1), custom_call_target="tpu_custom_call" | custom-call | flops 4294967296 | bytes 8388608 | tf_op jit(solution)/shard_map/whiten_own/pallas_call | solution.py:230
  18.4 8.8 %collective-permute-done.1.far_flag_ref.x_ref.prior_ref = bf16[65,8,1024]{2,1,0:T(8,128)(2,1)S(1)} collective-permute-done((bf16[65,8,1024]{2,1,0:T(8,128)(2,1)S(1)}, bf16[65,8,1024]{2,1,0:T(8,128)(2,1)S(1)}, u32[]{:S(2)}, u32[]{:S(2)}) %collective-permute-start.1) | collective-permute-done | bytes 1064992 | tf_op jit(solution)/shard_map/ppermute | solution.py:206
  27.3 0.0 copy-done.2
  27.3 14.9 %round_1.1.rest_0_ = bf16[2,64,64,512]{3,2,1,0:T(8,128)(2,1)} custom-call(bf16[65,8,1024]{2,1,0:T(8,128)(2,1)S(1)} %pad_maximum_fusion.flag_ref.prior_ref, bf16[65,8,1024]{2,1,0:T(8,128)(2,1)S(1)} %collective-permute-done.1.far_flag_ref.x_ref.prior_ref, bf16[65,8,1024]{2,1,0:T(8,128)(2,1)S(1)} %collective-permute-done.1.far_flag_ref.x_ref.prior_ref, ...), custom_call_target="tpu_custom_call" | custom-call | flops 17179869184 | bytes 16777216 | tf_op jit(solution)/shard_map/round_1/pallas_call | solution.py:266
  42.1 0.0 collective-permute-done.far_flag_ref.x_ref
  42.1 14.9 %round_2.1 = bf16[2,64,64,512]{3,2,1,0:T(8,128)(2,1)} custom-call(bf16[65,8,1024]{2,1,0:T(8,128)(2,1)S(1)} %pad_maximum_fusion.flag_ref.prior_ref, bf16[65,8,1024]{2,1,0:T(8,128)(2,1)S(1)} %collective-permute-done.far_flag_ref.x_ref, bf16[65,8,1024]{2,1,0:T(8,128)(2,1)S(1)} %collective-permute-done.far_flag_ref.x_ref, ...), custom_call_target="tpu_custom_call", output_to_operand_aliasing={{}: (7, {})} | custom-call | flops 17179869184 | bytes 16777216 | tf_op jit(solution)/shard_map/round_2/pallas_call | solution.py:266
  (1 shorter events, 0.0 us)
Async XLA Ops:
  0.7 1.5 %copy-start = (bf16[64,8,1024]{2,1,0:T(8,128)(2,1)S(1)}, bf16[64,8,1024]{2,1,0:T(8,128)(2,1)}, u32[]{:S(2)}) copy-start(bf16[64,8,1024]{2,1,0:T(8,128)(2,1)} %x_ref.1) | copy-start | bytes 3145732
  2.1 25.1 %collective-permute-start.1 = (bf16[65,8,1024]{2,1,0:T(8,128)(2,1)S(1)}, bf16[65,8,1024]{2,1,0:T(8,128)(2,1)S(1)}, u32[]{:S(2)}, u32[]{:S(2)}) collective-permute-start(bf16[65,8,1024]{2,1,0:T(8,128)(2,1)S(1)} %pad_maximum_fusion.flag_ref.prior_ref), channel_id=1, source_target_pairs={{1,0},{2,1},{3,2},{4,3},{5,4},{6,5},{7,6},{8,7},{9,8},{10,9},{11,1... | collective-permute-start | bytes 3194888 | tf_op jit(solution)/shard_map/ppermute | solution.py:206
  2.3 9.5 %collective-permute-start.2 = (bf16[1,8,1024]{2,1,0:T(8,128)(2,1)S(1)}, bf16[1,8,1024]{2,1,0:T(8,128)(2,1)S(1)}, u32[]{:S(2)}, u32[]{:S(2)}) collective-permute-start(bf16[1,8,1024]{2,1,0:T(8,128)(2,1)S(1)} %slice.3), channel_id=1, source_target_pairs={{15,0},{0,1},{1,2},{2,3},{3,4},{4,5},{5,6},{6,7},{7,8},{8,9},{9,10... | collective-permute-start | bytes 49160 | tf_op jit(solution)/shard_map/ppermute | solution.py:206
  4.9 37.2 %collective-permute-start = (bf16[65,8,1024]{2,1,0:T(8,128)(2,1)S(1)}, bf16[65,8,1024]{2,1,0:T(8,128)(2,1)S(1)}, u32[]{:S(2)}, u32[]{:S(2)}) collective-permute-start(bf16[65,8,1024]{2,1,0:T(8,128)(2,1)S(1)} %pad_maximum_fusion.flag_ref.prior_ref), channel_id=1, source_target_pairs={{2,0},{3,1},{4,2},{5,3},{6,4},{7,5},{8,6},{9,7},{10,8},{11,9},{12,... | collective-permute-start | bytes 3194888 | tf_op jit(solution)/shard_map/ppermute | solution.py:206
  11.7 1.6 %copy-start.1 = (bf16[1024,1024]{1,0:T(8,128)(2,1)S(1)}, bf16[1024,1024]{1,0:T(8,128)(2,1)}, u32[]{:S(2)}) copy-start(bf16[1024,1024]{1,0:T(8,128)(2,1)} %constant.4.clone.table_hbm.table_ref) | copy-start | bytes 6291460
  13.3 13.9 %copy-start.2 = (bf16[1024,512]{1,0:T(8,128)(2,1)S(1)}, bf16[1024,512]{1,0:T(8,128)(2,1)}, u32[]{:S(2)}) copy-start(bf16[1024,512]{1,0:T(8,128)(2,1)} %constant.5.clone.inverse_ref) | copy-start | bytes 3145732

commit v5 on v4

--- a/solution.py
+++ b/solution.py
@@ -208,7 +208,15 @@
     before = behind(traces[ch - 1 :], -1)
     row = jnp.broadcast_to(valid.astype(jnp.bfloat16)[:, :, None], (1, windows, samples))
     tagged = jnp.concatenate([traces, row], axis=0)
-    blocks = [tagged] + [behind(tagged, r) for r in range(1, ROUNDS + 1)]
+    near = behind(tagged, 1)
+    later, near = lax.optimization_barrier((tagged, near))
+    if n % 2 == 0:
+        relayed = lax.ppermute(near, "blk", [(i + 1, i) for i in range(0, n, 2)])
+        direct = lax.ppermute(later, "blk", [((i + 2) % n, i) for i in range(1, n, 2)])
+        second = jnp.where(lax.axis_index("blk") % 2 == 0, relayed, direct)
+    else:
+        second = behind(later, 2)
+    blocks = [tagged, near, second]
     table = forward_table(samples)
     inverse = inverse_table(samples)
 

time: 58.1 us -> 57.9 us (level); the launches traced: 57 us -> 57.6 us
  starting transfers between devices: 9.53 us -> 12.7 us
  waiting for transfers between devices: 8.85 us -> 6.08 us
    ppermute x0 -> x2, starting transfers between devices: none -> 9.99 us  [the longest x1 8.64 us: shards(): lax.ppermute(later, 'blk', [((i + 2) % n, i) for i in range(1, n, 2)])]
    ppermute x3 -> x2, starting transfers between devices: 9.53 us -> 2.69 us  [behind(): lax.ppermute(value, 'blk', [((i + distance) % n, i) for i in range(n)])]
    ppermute x3 -> x2, waiting for transfers between devices: 8.85 us -> 6.07 us  [behind(): lax.ppermute(value, 'blk', [((i + distance) % n, i) for i in range(n)])]
  transfers between devices with their start and end apart: 3 -> 4, of which waited for: 1 -> 2; matrix products, arithmetic and copies ran while one was open for 0% -> 0% of each run, Pallas kernels for 35% -> 35%
where the time goes in v5:
time: 57.9 us; the launch traced here: 57.6 us
  Pallas kernels  34.9 us (60%)
  starting transfers between devices  12.7 us (22%)
  waiting for transfers between devices  6.08 us (11%)
  other arithmetic  2.18 us (4%)
  local copies, waits for them, and re-layouts  1.73 us (3%)
    pallas_call x2, Pallas kernels, shards(): pl.pallas_call(functools.partial(round_kernel, r, n), grid=(stages,), out...  29.8 us
    ppermute x1, starting transfers between devices, shards(): lax.ppermute(later, 'blk', [((i + 2) % n, i) for i in range(1, n, 2)])  8.64 us
    ppermute x2, waiting for transfers between devices, behind(): lax.ppermute(value, 'blk', [((i + distance) % n, i) for i in range(n)])  6.07 us
    pallas_call x1, Pallas kernels, shards(): pl.pallas_call(own_kernel, out_shape=jax.ShapeDtypeStruct((bins // GROUP,...  5.07 us
    ppermute x2, starting transfers between devices, behind(): lax.ppermute(value, 'blk', [((i + distance) % n, i) for i in range(n)])  2.69 us
    unnamed x6, local copies, waits for them, and re-layouts  1.66 us
    concatenate x1, other arithmetic, shards(): tagged = jnp.concatenate([traces, row], axis=0)  1.41 us
    ppermute x1, starting transfers between devices, shards(): relayed = lax.ppermute(near, 'blk', [(i + 1, i) for i in range(0, n, 2)])  1.36 us
  transfers between devices with their start and end apart: 4, of which 2 were waited for; matrix products, arithmetic and copies ran while one was open for 0% of the time, Pallas kernels for 35%

profile of v5, /device:TPU:1, one launch (start us, length us, event | category | flops | bytes accessed | tf_op | source)
XLA Modules:
  0.0 57.6 jit_solution(13029976917996407310)
XLA Ops:
  0.0 0.7 %convert_bitcast_fusion = bf16[8]{0:T(256)(128)(2,1)S(1)} fusion(s32[1,8]{1,0:T(1,128)} %param.5), kind=kLoop, calls=%fused_computation.2 | loop fusion | flops 8 | bytes 48 | tf_op jit(solution)/shard_map/broadcast_in_dim | solution.py:209
  0.7 0.1 broadcast_in_dim.12
  0.7 0.0 copy-start
  0.7 1.4 %pad_maximum_fusion.flag_ref.prior_ref = bf16[65,8,1024]{2,1,0:T(8,128)(2,1)S(1)} fusion(bf16[1,8,1024]{2,1,0:T(8,128)(2,1)S(1)} %broadcast_in_dim.12, bf16[64,8,1024]{2,1,0:T(8,128)(2,1)} %x_ref.1), kind=kLoop, calls=%fused_computation | loop fusion | flops 532480 | bytes 2129920 | tf_op jit(solution)/shard_map/concatenate | solution.py:210
  2.1 0.1 collective-permute-start
  2.2 0.1 copy-done
  2.3 2.6 %collective-permute-start.3 = (bf16[1,8,1024]{2,1,0:T(8,128)(2,1)S(1)}, bf16[1,8,1024]{2,1,0:T(8,128)(2,1)S(1)}, u32[]{:S(2)}, u32[]{:S(2)}) collective-permute-start(bf16[1,8,1024]{2,1,0:T(8,128)(2,1)S(1)} %slice.3), channel_id=1, source_target_pairs={{15,0},{0,1},{1,2},{2,3},{3,4},{4,5},{5,6},{6,7},{7,8},{8,9},{9,10... | collective-permute-start | bytes 49160 | tf_op jit(solution)/shard_map/ppermute | solution.py:206
  4.9 3.5 %collective-permute-done.3.prior_ref = bf16[1,8,1024]{2,1,0:T(8,128)(2,1)S(1)} collective-permute-done((bf16[1,8,1024]{2,1,0:T(8,128)(2,1)S(1)}, bf16[1,8,1024]{2,1,0:T(8,128)(2,1)S(1)}, u32[]{:S(2)}, u32[]{:S(2)}) %collective-permute-start.3) | collective-permute-done | bytes 16416 | tf_op jit(solution)/shard_map/ppermute | solution.py:206
  8.4 0.0 copy-start.1
  8.4 1.6 %copy-done.1 = bf16[1024,1024]{1,0:T(8,128)(2,1)S(1)} copy-done((bf16[1024,1024]{1,0:T(8,128)(2,1)S(1)}, bf16[1024,1024]{1,0:T(8,128)(2,1)}, u32[]{:S(2)}) %copy-start.1) | copy-done | bytes 2097176
  10.0 0.0 copy-start.2
  10.0 5.1 %whiten_own.1.own_ref = bf16[64,64,128]{2,1,0:T(8,128)(2,1)S(1)} custom-call(bf16[64,8,1024]{2,1,0:T(8,128)(2,1)S(1)} %copy-done, bf16[1,8,1024]{2,1,0:T(8,128)(2,1)S(1)} %collective-permute-done.3.prior_ref, bf16[65,8,1024]{2,1,0:T(8,128)(2,1)S(1)} %pad_maximum_fusion.flag_ref.prior_ref, bf16[1024,1024]{1,0:T(8,128)(2,1)S(1)} %copy-done.1), custom_call_target="tpu_custom_call" | custom-call | flops 4294967296 | bytes 8388608 | tf_op jit(solution)/shard_map/whiten_own/pallas_call | solution.py:238
  15.0 2.6 %collective-permute-done.far_flag_ref.x_ref.prior_ref = bf16[65,8,1024]{2,1,0:T(8,128)(2,1)S(1)} collective-permute-done((bf16[65,8,1024]{2,1,0:T(8,128)(2,1)S(1)}, bf16[65,8,1024]{2,1,0:T(8,128)(2,1)S(1)}, u32[]{:S(2)}, u32[]{:S(2)}) %collective-permute-start) | collective-permute-done | bytes 1064992 | tf_op jit(solution)/shard_map/ppermute | solution.py:206
  17.7 8.6 %collective-permute-start.2 = (bf16[65,8,1024]{2,1,0:T(8,128)(2,1)S(1)}, bf16[65,8,1024]{2,1,0:T(8,128)(2,1)S(1)}, u32[]{:S(2)}, u32[]{:S(2)}) collective-permute-start(bf16[65,8,1024]{2,1,0:T(8,128)(2,1)S(1)} %pad_maximum_fusion.flag_ref.prior_ref), channel_id=1, source_target_pairs={{3,1},{5,3},{7,5},{9,7},{11,9},{13,11},{15,13},{1,15},{19,17},{21,... | collective-permute-start | bytes 3194888 | tf_op jit(solution)/shard_map/ppermute | solution.py:215
  26.3 1.4 %collective-permute-start.1 = (bf16[65,8,1024]{2,1,0:T(8,128)(2,1)S(1)}, bf16[65,8,1024]{2,1,0:T(8,128)(2,1)S(1)}, u32[]{:S(2)}, u32[]{:S(2)}) collective-permute-start(bf16[65,8,1024]{2,1,0:T(8,128)(2,1)S(1)} %collective-permute-done.far_flag_ref.x_ref.prior_ref), channel_id=1, source_target_pairs={{1,0},{3,2},{5,4},{7,6},{9,8},{11,10},{13,12},{15,14},{17,16},{19,... | collective-permute-start | bytes 3194888 | tf_op jit(solution)/shard_map/ppermute | solution.py:214
  27.7 0.0 copy-done.2
  27.7 14.9 %round_1.1.rest_0_ = bf16[2,64,64,512]{3,2,1,0:T(8,128)(2,1)} custom-call(bf16[65,8,1024]{2,1,0:T(8,128)(2,1)S(1)} %pad_maximum_fusion.flag_ref.prior_ref, bf16[65,8,1024]{2,1,0:T(8,128)(2,1)S(1)} %collective-permute-done.far_flag_ref.x_ref.prior_ref, bf16[65,8,1024]{2,1,0:T(8,128)(2,1)S(1)} %collective-permute-done.far_flag_ref.x_ref.prior_ref, ...), custom_call_target="tpu_custom_call" | custom-call | flops 17179869184 | bytes 16777216 | tf_op jit(solution)/shard_map/round_1/pallas_call | solution.py:274
  42.6 0.0 collective-permute-done.2
  42.6 0.0 collective-permute-done.1
  42.6 0.1 broadcast_select_fusion.far_flag_ref.x_ref
  42.7 14.9 %round_2.1 = bf16[2,64,64,512]{3,2,1,0:T(8,128)(2,1)} custom-call(bf16[65,8,1024]{2,1,0:T(8,128)(2,1)S(1)} %pad_maximum_fusion.flag_ref.prior_ref, bf16[65,8,1024]{2,1,0:T(8,128)(2,1)S(1)} %broadcast_select_fusion.far_flag_ref.x_ref, bf16[65,8,1024]{2,1,0:T(8,128)(2,1)S(1)} %broadcast_select_fusion.far_flag_ref.x_ref, ...), custom_call_target="tpu_custom_call", output_to_operand_aliasing={{}: (7, {})} | custom-call | flops 17179869184 | bytes 16777216 | tf_op jit(solution)/shard_map/round_2/pallas_call | solution.py:274
  (1 shorter events, 0.0 us)
Async XLA Ops:
  0.7 1.5 %copy-start = (bf16[64,8,1024]{2,1,0:T(8,128)(2,1)S(1)}, bf16[64,8,1024]{2,1,0:T(8,128)(2,1)}, u32[]{:S(2)}) copy-start(bf16[64,8,1024]{2,1,0:T(8,128)(2,1)} %x_ref.1) | copy-start | bytes 3145732
  2.1 15.5 %collective-permute-start = (bf16[65,8,1024]{2,1,0:T(8,128)(2,1)S(1)}, bf16[65,8,1024]{2,1,0:T(8,128)(2,1)S(1)}, u32[]{:S(2)}, u32[]{:S(2)}) collective-permute-start(bf16[65,8,1024]{2,1,0:T(8,128)(2,1)S(1)} %pad_maximum_fusion.flag_ref.prior_ref), channel_id=1, source_target_pairs={{1,0},{2,1},{3,2},{4,3},{5,4},{6,5},{7,6},{8,7},{9,8},{10,9},{11,1... | collective-permute-start | bytes 3194888 | tf_op jit(solution)/shard_map/ppermute | solution.py:206
  2.3 6.1 %collective-permute-start.3 = (bf16[1,8,1024]{2,1,0:T(8,128)(2,1)S(1)}, bf16[1,8,1024]{2,1,0:T(8,128)(2,1)S(1)}, u32[]{:S(2)}, u32[]{:S(2)}) collective-permute-start(bf16[1,8,1024]{2,1,0:T(8,128)(2,1)S(1)} %slice.3), channel_id=1, source_target_pairs={{15,0},{0,1},{1,2},{2,3},{3,4},{4,5},{5,6},{6,7},{7,8},{8,9},{9,10... | collective-permute-start | bytes 49160 | tf_op jit(solution)/shard_map/ppermute | solution.py:206
  8.4 1.6 %copy-start.1 = (bf16[1024,1024]{1,0:T(8,128)(2,1)S(1)}, bf16[1024,1024]{1,0:T(8,128)(2,1)}, u32[]{:S(2)}) copy-start(bf16[1024,1024]{1,0:T(8,128)(2,1)} %constant.22.clone.table_hbm.table_ref) | copy-start | bytes 6291460
  10.0 17.7 %copy-start.2 = (bf16[1024,512]{1,0:T(8,128)(2,1)S(1)}, bf16[1024,512]{1,0:T(8,128)(2,1)}, u32[]{:S(2)}) copy-start(bf16[1024,512]{1,0:T(8,128)(2,1)} %constant.23.clone.inverse_ref) | copy-start | bytes 3145732
  17.7 24.9 %collective-permute-start.2 = (bf16[65,8,1024]{2,1,0:T(8,128)(2,1)S(1)}, bf16[65,8,1024]{2,1,0:T(8,128)(2,1)S(1)}, u32[]{:S(2)}, u32[]{:S(2)}) collective-permute-start(bf16[65,8,1024]{2,1,0:T(8,128)(2,1)S(1)} %pad_maximum_fusion.flag_ref.prior_ref), channel_id=1, source_target_pairs={{3,1},{5,3},{7,5},{9,7},{11,9},{13,11},{15,13},{1,15},{19,17},{21,... | collective-permute-start | bytes 3194888 | tf_op jit(solution)/shard_map/ppermute | solution.py:215
  26.3 16.3 %collective-permute-start.1 = (bf16[65,8,1024]{2,1,0:T(8,128)(2,1)S(1)}, bf16[65,8,1024]{2,1,0:T(8,128)(2,1)S(1)}, u32[]{:S(2)}, u32[]{:S(2)}) collective-permute-start(bf16[65,8,1024]{2,1,0:T(8,128)(2,1)S(1)} %collective-permute-done.far_flag_ref.x_ref.prior_ref), channel_id=1, source_target_pairs={{1,0},{3,2},{5,4},{7,6},{9,8},{11,10},{13,12},{15,14},{17,16},{19,... | collective-permute-start | bytes 3194888 | tf_op jit(solution)/shard_map/ppermute | solution.py:214
